TPU v7x, 32 devices: a whole 2x2x4 slice. The times are simulated.
32 devices in a mesh: seq: 8 (over z, y), tensor: 4 (over x, core).
Axes of the slice: x: 2, y: 2, z: 4, core: 2. Of those that a mesh axis runs over, the one named last changes fastest.
Arguments:
- hidden_in: bfloat16 [1024, 2048], P('seq'), may hold values from -6 to 6
- norm_gain: float32 [2048], replicated, may hold values from 0.1 to 1.9
- query_weight: bfloat16 [2048, 2048], P(None, 'tensor'), may hold values from -0.125 to 0.125
- key_weight: bfloat16 [2048, 1024], P(None, 'tensor'), may hold values from -0.375 to 0.375
- value_weight: bfloat16 [2048, 1024], P(None, 'tensor'), may hold values from -0.125 to 0.125
- out_weight: bfloat16 [2048, 2048], P('tensor'), may hold values from -0.125 to 0.125
- key_cache: bfloat16 [512, 128, 1024], P('seq', None, 'tensor'), may hold values from -102 to 102
- value_cache: bfloat16 [512, 128, 1024], P('seq', None, 'tensor'), may hold values from -6 to 6
- cached_lengths: int32 [2], replicated, may hold values from 16385 to 32768, as said below
- group_ids: int32 [2], replicated, may hold values from 0 to 1
- prompt_pages: int32 [2, 128], replicated, may hold values from 0 to 511, as said below
- own_pages: int32 [2, 128], replicated, may hold values from 0 to 511, as said below
Outputs:
- attention_out: bfloat16 [1024, 2048], P('seq', 'tensor')
Inputs may be any that keep to these rules, and one draw needn't show every extreme that they name: `cached_lengths`: each request's cache holds the 16384 tokens of its group's prompt followed by its own tokens; some request holds the most in every draw. Slot s is page s % 64 of seq index s // 64; no slot is named twice in prompt_pages and own_pages together. `own_pages`: page p of request r holds its own cached tokens from p * 128 on; entries past a request's length name slots whose contents are not read.
All inputs are finite; a program needn't handle non-finite values.
Results may differ from a plain program's by a relative error of at most 0.0055.
The roundings to bfloat16 on the way count: a program that leaves them out, or rounds other values in their place, can miss the bound.
Values may be sent and summed in bfloat16 or wider, within the bound.
A program may use at most 64 MiB of HBM per device.

v0:
```python
import math

import jax
import jax.numpy as jnp
from jax import lax
from jax.sharding import PartitionSpec as P

HEAD_DIM = 128
PAGE_ROWS = 128
ADDED_TOKENS = 512
GROUPS = 2
PROMPT_PAGES = 128


def attend(query_grid, block_keys, block_values, live_mask, kv_dev, score_scale):
    key_grid = block_keys.reshape(PAGE_ROWS, kv_dev, HEAD_DIM)
    value_grid = block_values.reshape(PAGE_ROWS, kv_dev, HEAD_DIM)
    scores = (
        jnp.einsum("kgqd,pkd->kgqp", query_grid, key_grid, preferred_element_type=jnp.float32)
        * score_scale
    )
    live_grid = live_mask[None, None, :, :]
    block_max = jnp.max(jnp.where(live_grid, scores, -1e30), axis=-1)
    weights = jnp.exp(jnp.where(live_grid, scores - block_max[..., None], -1e30)).astype(
        jnp.bfloat16
    )
    block_sum = jnp.sum(weights.astype(jnp.float32), axis=-1)
    block_out = jnp.einsum(
        "kgqp,pkd->kgqd", weights, value_grid, preferred_element_type=jnp.float32
    )
    return (block_max, block_out, block_sum)


def combine_terms(running, terms):
    run_max, run_num, run_den = running
    part_max, part_num, part_den = terms
    new_max = jnp.maximum(run_max, part_max)
    keep_scale = jnp.exp(run_max - new_max)
    add_scale = jnp.exp(part_max - new_max)
    return (
        new_max,
        run_num * keep_scale[..., None] + part_num * add_scale[..., None],
        run_den * keep_scale + part_den * add_scale,
    )


def merge_rows(running, row_start, terms):
    row_count = terms[0].shape[2]
    current = tuple(
        (lax.dynamic_slice_in_dim(member, row_start, row_count, 2) for member in running)
    )
    merged = combine_terms(current, terms)
    return tuple(
        (
            lax.dynamic_update_slice_in_dim(member, updated, row_start, 2)
            for member, updated in zip(running, merged)
        )
    )


def body(
    hidden_in,
    norm_gain,
    query_weight,
    key_weight,
    value_weight,
    out_weight,
    key_cache,
    value_cache,
    cached_lengths,
    group_ids,
    prompt_pages,
    own_pages,
):
    tok_rows = hidden_in.shape[0]
    seq_count = lax.axis_size("seq")
    seq_index = lax.axis_index("seq")
    heads_dev = query_weight.shape[1] // HEAD_DIM
    kv_dev = key_weight.shape[1] // HEAD_DIM
    per_kv = heads_dev // kv_dev
    pages_dev = key_cache.shape[0]
    score_scale = 1.0 / math.sqrt(HEAD_DIM)
    floats = hidden_in.astype(jnp.float32)
    normed = (
        floats * lax.rsqrt(jnp.mean(floats * floats, axis=-1, keepdims=True) + 1e-05) * norm_gain
    ).astype(jnp.bfloat16)
    queries = jnp.dot(normed, query_weight, preferred_element_type=jnp.float32).astype(jnp.bfloat16)
    keys_new = jnp.dot(normed, key_weight, preferred_element_type=jnp.float32).astype(jnp.bfloat16)
    values_new = jnp.dot(normed, value_weight, preferred_element_type=jnp.float32).astype(
        jnp.bfloat16
    )
    all_queries, all_keys, all_values = (
        lax.all_gather(queries, "seq", axis=0, tiled=True),
        lax.all_gather(keys_new, "seq", axis=0, tiled=True),
        lax.all_gather(values_new, "seq", axis=0, tiled=True),
    )
    total_rows = all_queries.shape[0]
    query_heads = all_queries.reshape(total_rows, kv_dev, per_kv, HEAD_DIM).transpose(1, 2, 0, 3)
    running = (
        jnp.full((kv_dev, per_kv, total_rows), -1e30, jnp.float32),
        jnp.zeros((kv_dev, per_kv, total_rows, HEAD_DIM), jnp.float32),
        jnp.zeros((kv_dev, per_kv, total_rows), jnp.float32),
    )
    own_len = cached_lengths - PROMPT_PAGES * PAGE_ROWS
    onehot = (group_ids[:, None] == jnp.arange(GROUPS, dtype=jnp.int32)[None, :]).astype(jnp.int32)
    request_prompt = jnp.sum(onehot[:, :, None] * prompt_pages[None, :, :], axis=1)
    slot_table = jnp.concatenate([request_prompt, own_pages], axis=1)
    blocks_all = slot_table.shape[1]
    block_pos = jnp.arange(blocks_all, dtype=jnp.int32)[None, :]
    live_table = jnp.where(
        block_pos < PROMPT_PAGES,
        PAGE_ROWS,
        jnp.clip(own_len[:, None] - (block_pos - PROMPT_PAGES) * PAGE_ROWS, 0, PAGE_ROWS),
    )
    owned = (slot_table // pages_dev == seq_index) & (live_table > 0)
    flat_owned = owned.reshape(-1)
    entry_count = jnp.sum(flat_owned.astype(jnp.int32))
    entry_list = jnp.nonzero(flat_owned, size=flat_owned.shape[0], fill_value=0)[0].astype(
        jnp.int32
    )
    flat_slots = slot_table.reshape(-1)
    flat_live = live_table.reshape(-1)
    key_pos = jnp.arange(PAGE_ROWS, dtype=jnp.int32)

    def cache_entry(position, running):
        entry_id = entry_list[position]
        request = entry_id // blocks_all
        local_page = flat_slots[entry_id] - seq_index * pages_dev
        live_mask = jnp.broadcast_to(
            (key_pos < flat_live[entry_id])[None, :], (ADDED_TOKENS, PAGE_ROWS)
        )
        query_grid = lax.dynamic_slice_in_dim(query_heads, request * ADDED_TOKENS, ADDED_TOKENS, 2)
        page_keys = lax.dynamic_index_in_dim(key_cache, local_page, 0, keepdims=False)
        page_values = lax.dynamic_index_in_dim(value_cache, local_page, 0, keepdims=False)
        terms = attend(query_grid, page_keys, page_values, live_mask, kv_dev, score_scale)
        return merge_rows(running, request * ADDED_TOKENS, terms)

    running = lax.fori_loop(0, entry_count, cache_entry, running)
    my_start = seq_index * tok_rows
    home_request = my_start // ADDED_TOKENS
    query_pos = my_start - home_request * ADDED_TOKENS + jnp.arange(tok_rows, dtype=jnp.int32)
    home_keys = lax.dynamic_slice_in_dim(all_keys, home_request * ADDED_TOKENS, ADDED_TOKENS, 0)
    home_values = lax.dynamic_slice_in_dim(all_values, home_request * ADDED_TOKENS, ADDED_TOKENS, 0)
    my_queries = lax.dynamic_slice_in_dim(query_heads, my_start, tok_rows, 2)
    for block_index in range(ADDED_TOKENS // PAGE_ROWS):
        key_start = block_index * PAGE_ROWS
        live_mask = (key_start + key_pos)[None, :] <= query_pos[:, None]
        terms = attend(
            my_queries,
            home_keys[key_start : key_start + PAGE_ROWS],
            home_values[key_start : key_start + PAGE_ROWS],
            live_mask,
            kv_dev,
            score_scale,
        )
        running = merge_rows(running, my_start, terms)
    run_max, run_num, run_den = running
    den_safe = jnp.maximum(run_den, 1.0)
    partial_value = (
        (run_num / den_safe[..., None])
        .astype(jnp.bfloat16)
        .reshape(heads_dev, total_rows, HEAD_DIM)
    )
    log_scale = (run_max + jnp.log(den_safe)).reshape(heads_dev, total_rows)
    got_part = lax.all_to_all(
        partial_value.reshape(heads_dev, seq_count, tok_rows, HEAD_DIM),
        "seq",
        split_axis=1,
        concat_axis=1,
        tiled=True,
    )
    got_scale = lax.all_to_all(
        log_scale.reshape(heads_dev, seq_count, tok_rows),
        "seq",
        split_axis=1,
        concat_axis=1,
        tiled=True,
    )
    highest = jnp.max(got_scale, axis=1)
    scale_weights = jnp.exp(got_scale - highest[:, None])
    attention = (
        jnp.sum(got_part.astype(jnp.float32) * scale_weights[..., None], axis=1)
        / jnp.sum(scale_weights, axis=1)[..., None]
    )
    attention = (
        attention.transpose(1, 0, 2).reshape(tok_rows, heads_dev * HEAD_DIM).astype(jnp.bfloat16)
    )
    head_terms = jnp.dot(attention, out_weight, preferred_element_type=jnp.float32)
    return lax.psum_scatter(head_terms, "tensor", scatter_dimension=1, tiled=True).astype(
        jnp.bfloat16
    )


def solution(mesh):
    in_specs = (
        P("seq", None),
        P(),
        P(None, "tensor"),
        P(None, "tensor"),
        P(None, "tensor"),
        P("tensor", None),
        P("seq", None, "tensor"),
        P("seq", None, "tensor"),
        P(),
        P(),
        P(),
        P(),
    )
    out_specs = P("seq", "tensor")
    return jax.shard_map(body, mesh=mesh, in_specs=in_specs, out_specs=out_specs, check_vma=False)
```

profile of v0, /device:TPU:0, one launch (start us, length us, event | category | flops | bytes accessed | tf_op | source)
XLA Modules:
  0.0 1217.2 jit_solution(4031724688622249589)
XLA Ops:
  8.0 2.9 convolution_convert_fusion
  14.3 34.0 %all_gather.10 = bf16[1024,256]{1,0:T(8,128)(2,1)S(1)} all-gather(bf16[128,256]{1,0:T(8,128)(2,1)S(1)} %convolution_convert_fusion.2), channel_id=1, replica_groups=mesh['seq'=8,'tensor'=4] {'seq'}, dimensions={0}, use_global_device_ids=true | all-gather | bytes 589824 | tf_op jit(solution)/shard_map/all_gather | solution.py:94
  48.4 4.1 scatter_custom_fusion
  56.3 31.2 %all_gather.11 = bf16[1024,256]{1,0:T(8,128)(2,1)S(1)} all-gather(bf16[128,256]{1,0:T(8,128)(2,1)S(1)} %convolution_convert_fusion.1), channel_id=1, replica_groups=mesh['seq'=8,'tensor'=4] {'seq'}, dimensions={0}, use_global_device_ids=true | all-gather | bytes 589824 | tf_op jit(solution)/shard_map/all_gather | solution.py:95
  95.6 867.3 %while.17 = (s32[]{:T(128)}, f32[2,2,1024]{2,1,0:T(2,128)S(1)}, f32[2,2,1024,128]{3,2,1,0:T(8,128)}, f32[2,2,1024]{2,1,0:T(2,128)S(1)}, s32[]{:T(128)}, /*index=...) while((s32[]{:T(128)}, f32[2,2,1024]{2,1,0:T(2,128)S(1)}, ...), condition=%wide.region_11.12_spmd.clone, body=%wide.region_8.11_spmd.clone.sunk | while | flops 137896096 | bytes 6538274 | solution.py:138
  547.7 2.9 fusion.83
  562.4 2.9 fusion.83
  577.1 2.9 fusion.83
  591.8 2.9 fusion.83
  606.5 2.9 fusion.83
  621.2 2.9 fusion.83
  635.9 2.9 fusion.83
  650.6 2.9 fusion.83
  665.4 2.9 fusion.83
  680.1 2.9 fusion.83
  694.8 2.9 fusion.83
  709.5 2.9 fusion.83
  724.2 2.9 fusion.83
  738.9 2.9 fusion.83
  768.3 2.9 fusion.83
  783.0 2.9 fusion.83
  797.7 2.9 fusion.83
  812.4 2.9 fusion.83
  827.1 2.9 fusion.83
  841.8 2.9 fusion.83
  856.5 2.9 fusion.83
  871.2 2.9 fusion.83
  885.9 2.9 fusion.83
  971.7 177.3 %all-to-all-start.1 = ((f32[4,8,128]{2,0,1:T(4,128)}), f32[4,8,128]{2,0,1:T(4,128)S(1)}, u32[]{:S(2)}, u32[]{:S(2)}) async-start(f32[4,8,128]{2,0,1:T(4,128)} %copy.112), calls=%async_computation.1 | async-start | bytes 32768 | tf_op jit(solution)/shard_map/all_to_all | solution.py:172
  1159.8 6.1 all-to-all-start
  1166.0 16.3 %all-to-all-done = bf16[4,8,128,128]{3,2,0,1:T(8,128)(2,1)S(1)} async-done(((bf16[4,8,128,128]{3,2,0,1:T(8,128)(2,1)}), bf16[4,8,128,128]{3,2,0,1:T(8,128)(2,1)S(1)}, u32[]{:S(2)}, u32[]{:S(2)}) %all-to-all-start) | async-done | bytes 1048608 | tf_op jit(solution)/shard_map/all_to_all | solution.py:165
  1184.8 24.0 %reduce-scatter.2.cloned.1.call-done = f32[128,512]{1,0:T(8,128)} async-done(((f32[128,2048]{1,0:T(8,128)}), f32[128,512]{1,0:T(8,128)}) %reduce-scatter.2.cloned.1.call-update) | async-done | bytes 262160 | tf_op jit(solution)/shard_map/reduce_scatter | solution.py:189
  (747 shorter events, 534.1 us)
Async XLA Ops:
  6.5 1176.8 %copy-start = (bf16[512,2048]{1,0:T(8,128)(2,1)S(1)}, bf16[512,2048]{1,0:T(8,128)(2,1)}, u32[]{:S(2)}) copy-start(bf16[512,2048]{1,0:T(8,128)(2,1)} %param.19) | copy-start | bytes 6291460
  6.5 6.2 copy-start.1
  6.5 6.2 copy-start.15
  6.5 4.5 copy-start.16
  6.5 4.6 copy-start.17
  6.5 4.6 copy-start.13
  6.6 4.7 copy-start.14
  6.6 85.1 %all-gather.2.cloned.1.call-start = ((), (), s32[]{:S(2)}) async-start(), calls=%async_computation.3 | async-start | bytes 1179648 | tf_op jit(solution)/shard_map/all_gather | solution.py:93
  963.0 6.7 copy-start.3
  963.0 186.0 %copy-start.2 = (bf16[128,2,128]{2,1,0:T(2,128)(2,1)S(1)}, bf16[128,2,128]{2,1,0:T(2,128)(2,1)}, u32[]{:S(2)}) copy-start(bf16[128,2,128]{2,1,0:T(2,128)(2,1)} %reshape.325) | copy-start | bytes 196612
  963.0 186.0 %copy-start.5 = (pred[128,128]{0,1:T(8,128)(4,1)S(1)}, pred[128,128]{0,1:T(8,128)(4,1)}, u32[]{:S(2)}) copy-start(pred[128,128]{0,1:T(8,128)(4,1)} %get-tuple-element.321) | copy-start | bytes 49156
  963.0 188.0 %copy-start.4 = (pred[128,128]{0,1:T(8,128)(4,1)S(1)}, pred[128,128]{0,1:T(8,128)(4,1)}, u32[]{:S(2)}) copy-start(pred[128,128]{0,1:T(8,128)(4,1)} %get-tuple-element.319) | copy-start | bytes 49156
  964.2 6.8 copy-start.8
  965.3 5.7 copy-start.10
  966.4 4.6 copy-start.6
  967.6 3.5 copy-start.9
  971.0 183.8 %copy-start.11 = (f32[2,2,128]{2,1,0:T(2,128)S(1)}, f32[2,2,128]{2,1,0:T(2,128)}, u32[]{:S(2)}) copy-start(f32[2,2,128]{2,1,0:T(2,128)} %get-tuple-element.282) | copy-start | bytes 6148
  971.1 183.8 %copy-start.12 = (f32[2,2,128]{2,1,0:T(2,128)S(1)}, f32[2,2,128]{2,1,0:T(2,128)}, u32[]{:S(2)}) copy-start(f32[2,2,128]{2,1,0:T(2,128)} %get-tuple-element.283) | copy-start | bytes 6148
  971.1 183.8 %copy-start.7 = (f32[2,2,128]{2,1,0:T(2,128)S(1)}, f32[2,2,128]{2,1,0:T(2,128)}, u32[]{:S(2)}) copy-start(f32[2,2,128]{2,1,0:T(2,128)} %copy-done.6) | copy-start | bytes 6148
  971.7 188.1 %all-to-all-start.1 = ((f32[4,8,128]{2,0,1:T(4,128)}), f32[4,8,128]{2,0,1:T(4,128)S(1)}, u32[]{:S(2)}, u32[]{:S(2)}) async-start(f32[4,8,128]{2,0,1:T(4,128)} %copy.112), calls=%async_computation.1 | async-start | bytes 32768 | tf_op jit(solution)/shard_map/all_to_all | solution.py:172
  1159.8 22.5 %all-to-all-start = ((bf16[4,8,128,128]{3,2,0,1:T(8,128)(2,1)}), bf16[4,8,128,128]{3,2,0,1:T(8,128)(2,1)S(1)}, u32[]{:S(2)}, u32[]{:S(2)}) async-start(bf16[4,8,128,128]{3,2,0,1:T(8,128)(2,1)} %copy.111), calls=%async_computation | async-start | bytes 2097152 | tf_op jit(solution)/shard_map/all_to_all | solution.py:165
  1165.9 42.9 %reduce-scatter.2.cloned.1.call-start = ((), (), s32[]{:S(2)}) async-start(), calls=%async_computation.4 | async-start | bytes 1310720 | tf_op jit(solution)/shard_map/reduce_scatter | solution.py:189
Sparse Core Ops, SparseCore 0:
  11.1 45.3 all-gather.1
  1184.9 23.8 reduce-scatter.1
where the time goes:
time: 1200 us; the launch traced here: 1220 us
  loops' own time  306 us (26%)
  matrix products  276 us (23%)
  local copies, waits for them, and re-layouts  259 us (22%)
  starting transfers between devices  183 us (15%)
  other arithmetic  73.3 us (6%)
  blocking collectives  65.2 us (5%)
  waiting for transfers between devices  40.3 us (3%)
  between operations  13.8 us (1%)
    another operation x1, loops' own time, body(): running = lax.fori_loop(0, entry_count, cache_entry, running)  306 us
    dot_general x63, matrix products, attend(): jnp.einsum('kgqp,pkd->kgqd', weights, value_grid, preferred_element_type=...  180 us
    all_to_all x1, starting transfers between devices, body(): lax.all_to_all(log_scale.reshape(heads_dev, seq_count, tok_rows), 'seq',...  177 us
    dot_general x63, matrix products, attend(): jnp.einsum('kgqd,pkd->kgqp', query_grid, key_grid, preferred_element_type...  88.3 us
    dynamic_slice x59, local copies, waits for them, and re-layouts, cache_entry(): entry_id = entry_list[position]  75.1 us
    dynamic_slice x59, local copies, waits for them, and re-layouts, cache_entry(): local_page = flat_slots[entry_id] - seq_index * pages_dev  74 us
    dynamic_slice x118, local copies, waits for them, and re-layouts, cache_entry(): lax.dynamic_index_in_dim(value_cache, local_page, 0, keepdims=False)  58.8 us
    lt x59, other arithmetic, cache_entry(): key_pos < flat_live[entry_id]  38.3 us
  transfers between devices with their start and end apart: 4, of which 2 were waited for; matrix products, arithmetic and copies ran while one was open for 2% of the time, Pallas kernels for 0%

commit v1 on v0

v1 whole, which is shorter than its diff:
```python
import functools
import math

import jax
import jax.numpy as jnp
from jax import lax
from jax.experimental import pallas as pl
from jax.experimental.pallas import tpu as pltpu
from jax.sharding import PartitionSpec as P

HEAD_DIM = 128
PAGE_ROWS = 128
ADDED_TOKENS = 512
GROUPS = 2
PROMPT_PAGES = 128
STEP_PAGES = 4
ROW_CHUNK = 256
SCORE_SCALE = 1.0 / math.sqrt(HEAD_DIM)
EXP2_SCALE = SCORE_SCALE * math.log2(math.e)
EMPTY = -1e30


def dot_nt(left, right):
    return lax.dot_general(
        left, right, (((1,), (1,)), ((), ())), preferred_element_type=jnp.float32
    )


def attend_kernel(
    per_kv,
    tok_rows,
    entries,
    counts,
    meta,
    q_ref,
    kn_ref,
    vn_ref,
    kc_ref,
    vc_ref,
    o_ref,
    ls_ref,
    m_ref,
    acc_ref,
):
    request = pl.program_id(0)
    heads = o_ref.shape[0]
    kv_count = heads // per_kv
    m_ref[...] = jnp.full_like(m_ref, EMPTY)
    acc_ref[...] = jnp.zeros_like(acc_ref)

    def cols(index):
        return slice(index * HEAD_DIM, (index + 1) * HEAD_DIM)

    @pl.when(meta[0] == request)
    def _():
        start = pl.multiple_of(meta[1], tok_rows)
        row = lax.broadcasted_iota(jnp.int32, (tok_rows, ADDED_TOKENS), 0)
        col = lax.broadcasted_iota(jnp.int32, (tok_rows, ADDED_TOKENS), 1)
        live = col <= row + start
        ones = jnp.ones((ADDED_TOKENS, HEAD_DIM), jnp.bfloat16)
        for head in range(heads):
            kv = head // per_kv
            scores = dot_nt(q_ref[pl.ds(start, tok_rows), cols(head)], kn_ref[:, cols(kv)])
            scores = jnp.where(live, scores, EMPTY)
            top = jnp.max(scores, axis=1, keepdims=True)
            weights = jnp.exp2((scores - top) * EXP2_SCALE).astype(jnp.bfloat16)
            values = jnp.concatenate([vn_ref[:, cols(kv)], ones], axis=1)
            m_ref[head, pl.ds(start, tok_rows), :] = jnp.broadcast_to(top, (tok_rows, HEAD_DIM))
            acc_ref[head, pl.ds(start, tok_rows), :] = jnp.dot(
                weights, values, preferred_element_type=jnp.float32
            )

    def step(index, carry):
        picked = [entries[request, index * STEP_PAGES + j] for j in range(STEP_PAGES)]
        lane = lax.broadcasted_iota(jnp.int32, (1, PAGE_ROWS), 1)
        bias = jnp.concatenate(
            [jnp.where(lane < (item & 255), 0.0, EMPTY) for item in picked], axis=1
        )
        pages = [item >> 8 for item in picked]
        ones = jnp.ones((STEP_PAGES * PAGE_ROWS, HEAD_DIM), jnp.bfloat16)
        for kv in range(kv_count):
            keys = jnp.concatenate([kc_ref[page, :, cols(kv)] for page in pages], axis=0)
            values = jnp.concatenate([vc_ref[page, :, cols(kv)] for page in pages], axis=0)
            values = jnp.concatenate([values, ones], axis=1)
            for head in range(kv * per_kv, (kv + 1) * per_kv):
                for chunk in range(ADDED_TOKENS // ROW_CHUNK):
                    rows = slice(chunk * ROW_CHUNK, (chunk + 1) * ROW_CHUNK)
                    scores = dot_nt(q_ref[rows, cols(head)], keys) + bias
                    old = m_ref[head, rows, :]
                    new = jnp.maximum(old, jnp.max(scores, axis=1, keepdims=True))
                    weights = jnp.exp2(
                        (scores - jnp.tile(new, (1, STEP_PAGES))) * EXP2_SCALE
                    ).astype(jnp.bfloat16)
                    keep = jnp.exp2((old - new) * EXP2_SCALE)
                    m_ref[head, rows, :] = new
                    acc_ref[head, rows, :] = acc_ref[head, rows, :] * jnp.tile(
                        keep, (1, 2)
                    ) + jnp.dot(weights, values, preferred_element_type=jnp.float32)
        return carry

    lax.fori_loop(0, (counts[request] + STEP_PAGES - 1) // STEP_PAGES, step, 0)
    eye = lax.broadcasted_iota(jnp.int32, (128, 128), 0) == lax.broadcasted_iota(
        jnp.int32, (128, 128), 1
    )
    for head in range(heads):
        den = jnp.maximum(acc_ref[head, :, HEAD_DIM:], 1.0)
        o_ref[head] = (acc_ref[head, :, :HEAD_DIM] / den).astype(jnp.bfloat16)
        scale = m_ref[head] * SCORE_SCALE + jnp.log(den)
        for block in range(ADDED_TOKENS // 128):
            part = scale[block * 128 : (block + 1) * 128]
            ls_ref[0, head : head + 1, block * 128 : (block + 1) * 128] = jnp.sum(
                jnp.where(eye, part, 0.0), axis=0, keepdims=True
            )


def attend(entries, counts, meta, gathered, key_cache, value_cache, per_kv, tok_rows):
    total_rows = gathered.shape[0]
    requests = total_rows // ADDED_TOKENS
    kv_cols = key_cache.shape[2]
    heads = kv_cols // HEAD_DIM * per_kv
    q_cols = heads * HEAD_DIM
    whole = pl.BlockSpec(
        key_cache.shape, lambda r, e, c, m: (0, 0, 0), pipeline_mode=pl.Buffered(1)
    )
    pages = key_cache.shape[0]
    return pl.pallas_call(
        functools.partial(attend_kernel, per_kv, tok_rows),
        out_shape=(
            jax.ShapeDtypeStruct((heads, total_rows, HEAD_DIM), jnp.bfloat16),
            jax.ShapeDtypeStruct((requests, heads, ADDED_TOKENS), jnp.float32),
        ),
        grid_spec=pltpu.PrefetchScalarGridSpec(
            num_scalar_prefetch=3,
            grid=(requests,),
            in_specs=[
                pl.BlockSpec((ADDED_TOKENS, q_cols), lambda r, e, c, m: (r, 0)),
                pl.BlockSpec((ADDED_TOKENS, kv_cols), lambda r, e, c, m: (m[0], q_cols // kv_cols)),
                pl.BlockSpec(
                    (ADDED_TOKENS, kv_cols), lambda r, e, c, m: (m[0], q_cols // kv_cols + 1)
                ),
                whole,
                whole,
            ],
            out_specs=(
                pl.BlockSpec((heads, ADDED_TOKENS, HEAD_DIM), lambda r, e, c, m: (0, r, 0)),
                pl.BlockSpec((1, heads, ADDED_TOKENS), lambda r, e, c, m: (r, 0, 0)),
            ),
            scratch_shapes=[
                pltpu.VMEM((heads, ADDED_TOKENS, HEAD_DIM), jnp.float32),
                pltpu.VMEM((heads, ADDED_TOKENS, 2 * HEAD_DIM), jnp.float32),
            ],
        ),
        compiler_params=pltpu.CompilerParams(
            dimension_semantics=("arbitrary",), vmem_limit_bytes=48 << 20
        ),
        cost_estimate=pl.CostEstimate(
            flops=4 * pages * PAGE_ROWS * ADDED_TOKENS * q_cols,
            bytes_accessed=4 * pages * PAGE_ROWS * kv_cols,
            transcendentals=pages * PAGE_ROWS * ADDED_TOKENS * heads,
        ),
    )(entries, counts, meta, gathered, gathered, gathered, key_cache, value_cache)


def page_lists(cached_lengths, group_ids, prompt_pages, own_pages, pages_dev, seq_index):
    own_len = cached_lengths - PROMPT_PAGES * PAGE_ROWS
    onehot = (group_ids[:, None] == jnp.arange(GROUPS, dtype=jnp.int32)[None, :]).astype(jnp.int32)
    request_prompt = jnp.sum(onehot[:, :, None] * prompt_pages[None, :, :], axis=1)
    slots = jnp.concatenate([request_prompt, own_pages], axis=1)
    count = slots.shape[1]
    position = jnp.arange(count, dtype=jnp.int32)
    live = jnp.where(
        position[None, :] < PROMPT_PAGES,
        PAGE_ROWS,
        jnp.clip(own_len[:, None] - (position[None, :] - PROMPT_PAGES) * PAGE_ROWS, 0, PAGE_ROWS),
    )
    owned = (slots // pages_dev == seq_index) & (live > 0)
    marks = owned.astype(jnp.int32)
    before = jnp.sum(
        jnp.where(position[None, None, :] < position[None, :, None], marks[:, None, :], 0), axis=2
    )
    packed = (slots - seq_index * pages_dev) * 256 + live
    length = -(-pages_dev // STEP_PAGES) * STEP_PAGES
    places = jnp.arange(length, dtype=jnp.int32)
    entries = jnp.sum(
        jnp.where(
            owned[:, None, :] & (before[:, None, :] == places[None, :, None]),
            packed[:, None, :],
            0,
        ),
        axis=2,
    )
    return entries, jnp.sum(marks, axis=1)


def body(
    hidden_in,
    norm_gain,
    query_weight,
    key_weight,
    value_weight,
    out_weight,
    key_cache,
    value_cache,
    cached_lengths,
    group_ids,
    prompt_pages,
    own_pages,
):
    tok_rows = hidden_in.shape[0]
    seq_count = lax.axis_size("seq")
    seq_index = lax.axis_index("seq")
    heads_dev = query_weight.shape[1] // HEAD_DIM
    kv_dev = key_weight.shape[1] // HEAD_DIM
    per_kv = heads_dev // kv_dev
    floats = hidden_in.astype(jnp.float32)
    normed = (
        floats * lax.rsqrt(jnp.mean(floats * floats, axis=-1, keepdims=True) + 1e-05) * norm_gain
    ).astype(jnp.bfloat16)
    projected = [
        jnp.dot(normed, weight, preferred_element_type=jnp.float32).astype(jnp.bfloat16)
        for weight in (query_weight, key_weight, value_weight)
    ]
    gathered = lax.all_gather(jnp.concatenate(projected, axis=1), "seq", axis=0, tiled=True)
    entries, counts = page_lists(
        cached_lengths, group_ids, prompt_pages, own_pages, key_cache.shape[0], seq_index
    )
    my_start = seq_index * tok_rows
    home = my_start // ADDED_TOKENS
    meta = jnp.stack([home, my_start - home * ADDED_TOKENS]).astype(jnp.int32)
    partial_value, log_scale = attend(
        entries, counts, meta, gathered, key_cache, value_cache, per_kv, tok_rows
    )
    log_scale = log_scale.transpose(1, 0, 2)
    got_part = lax.all_to_all(
        partial_value.reshape(heads_dev, seq_count, tok_rows, HEAD_DIM),
        "seq",
        split_axis=1,
        concat_axis=1,
        tiled=True,
    )
    got_scale = lax.all_to_all(
        log_scale.reshape(heads_dev, seq_count, tok_rows),
        "seq",
        split_axis=1,
        concat_axis=1,
        tiled=True,
    )
    highest = jnp.max(got_scale, axis=1)
    scale_weights = jnp.exp(got_scale - highest[:, None])
    attention = (
        jnp.sum(got_part.astype(jnp.float32) * scale_weights[..., None], axis=1)
        / jnp.sum(scale_weights, axis=1)[..., None]
    )
    attention = (
        attention.transpose(1, 0, 2).reshape(tok_rows, heads_dev * HEAD_DIM).astype(jnp.bfloat16)
    )
    head_terms = jnp.dot(attention, out_weight, preferred_element_type=jnp.float32)
    return lax.psum_scatter(head_terms, "tensor", scatter_dimension=1, tiled=True).astype(
        jnp.bfloat16
    )


def solution(mesh):
    in_specs = (
        P("seq", None),
        P(),
        P(None, "tensor"),
        P(None, "tensor"),
        P(None, "tensor"),
        P("tensor", None),
        P("seq", None, "tensor"),
        P("seq", None, "tensor"),
        P(),
        P(),
        P(),
        P(),
    )
    out_specs = P("seq", "tensor")
    return jax.shard_map(body, mesh=mesh, in_specs=in_specs, out_specs=out_specs, check_vma=False)
```

time: 1200 us -> 171 us (0.14); the launches traced: 1220 us -> 169 us
  loops' own time: 306 us -> 0 us
  matrix products: 276 us -> 5.36 us
  local copies, waits for them, and re-layouts: 259 us -> 2.87 us
  starting transfers between devices: 183 us -> 6.94 us
  other arithmetic: 73.3 us -> 5.42 us
  blocking collectives: 65.2 us -> 0 us
  waiting for transfers between devices: 40.3 us -> 105 us
  Pallas kernels: 0 us -> 29.4 us
    another operation x1 -> x0, loops' own time: 306 us -> none  [body(): running = lax.fori_loop(0, entry_count, cache_entry, running)]
    dot_general x129 -> x3, matrix products: 274 us -> 3.9 us  [body(): jnp.dot(normed, weight, preferred_element_type=jnp.float32)]
    dynamic_slice x354 -> x0, local copies, waits for them, and re-layouts: 249 us -> none  [the longest x59 75.1 us: cache_entry(): entry_id = entry_list[position]]
    all_to_all x1, starting transfers between devices: 177 us -> 3.34 us  [body(): lax.all_to_all(log_scale.reshape(heads_dev, seq_count, tok_rows), 'seq',...]
    all_gather x2 -> x0, blocking collectives: 65.2 us -> none  [the longest x1 34 us: body(): lax.all_gather(keys_new, 'seq', axis=0, tiled=True)]
    all_gather x1, waiting for transfers between devices: 0.01 us -> 51.3 us  [body(): lax.all_gather(jnp.concatenate(projected, axis=1), 'seq', axis=0, tiled=T...]
    lt x61 -> x2, other arithmetic: 38.3 us -> 0.03 us  [the longest x1 0.03 us: page_lists(): position[None, None, :] < position[None, :, None]]
    pallas_call x0 -> x1, Pallas kernels: none -> 29.4 us  [attend(): pl.pallas_call(functools.partial(attend_kernel, per_kv, tok_rows), out_sh...]
  transfers between devices with their start and end apart: 4 -> 4, of which waited for: 2 -> 4; matrix products, arithmetic and copies ran while one was open for 2% -> 1% of each run, Pallas kernels for 0% -> 0%
where the time goes in v1:
time: 171 us; the launch traced here: 169 us
  waiting for transfers between devices  105 us (61%)
  Pallas kernels  29.4 us (17%)
  between operations  13.6 us (8%)
  starting transfers between devices  6.94 us (4%)
  other arithmetic  5.42 us (3%)
  matrix products  5.36 us (3%)
  local copies, waits for them, and re-layouts  2.87 us (2%)
    all_gather x1, waiting for transfers between devices, body(): lax.all_gather(jnp.concatenate(projected, axis=1), 'seq', axis=0, tiled=T...  51.3 us
    pallas_call x1, Pallas kernels, attend(): pl.pallas_call(functools.partial(attend_kernel, per_kv, tok_rows), out_sh...  29.4 us
    all_to_all x1, waiting for transfers between devices, body(): lax.all_to_all(partial_value.reshape(heads_dev, seq_count, tok_rows, HEAD...  24.4 us
    reduce_scatter x1, waiting for transfers between devices, body(): lax.psum_scatter(head_terms, 'tensor', scatter_dimension=1, tiled=True)  23.9 us
    all_to_all x1, waiting for transfers between devices, body(): lax.all_to_all(log_scale.reshape(heads_dev, seq_count, tok_rows), 'seq',...  5.41 us
    dot_general x3, matrix products, body(): jnp.dot(normed, weight, preferred_element_type=jnp.float32)  3.9 us
    all_to_all x1, starting transfers between devices, body(): lax.all_to_all(partial_value.reshape(heads_dev, seq_count, tok_rows, HEAD...  3.56 us
  transfers between devices with their start and end apart: 4, of which 4 were waited for; matrix products, arithmetic and copies ran while one was open for 1% of the time, Pallas kernels for 0%

profile of v1, /device:TPU:0, one launch (start us, length us, event | category | flops | bytes accessed | tf_op | source)
XLA Modules:
  0.0 168.6 jit_solution(16324250538682664722)
XLA Ops:
  6.6 1.4 fusion
  7.9 1.8 %convolution_convert_fusion.2 = bf16[128,256]{1,0:T(8,128)(2,1)S(1)} fusion(bf16[2048,256]{1,0:T(8,128)(2,1)} %param.15, bf16[128,2048]{1,0:T(8,128)(2,1)} %param.12, f32[2048]{0:T(1024)} %param.13, f32[128]{0:T(128)S(1)} %add_rsqrt_fusion), kind=kOutput, calls=%fused_computation.5 | convolution fusion | flops 135299072 | bytes 1647104 | tf_op jit(solution)/shard_map/dot_general | solution.py:220
  9.8 1.6 convolution_convert_fusion.1
  11.4 0.0 copy-start.7
  11.4 0.0 copy-start.3
  11.4 0.0 copy-start.8
  11.4 0.0 copy-start.4
  11.5 0.5 convolution_convert_fusion
  11.9 0.8 pad_maximum_fusion
  12.7 0.0 all-gather.2.cloned.1.call-update
  12.8 0.1 compare_convert_fusion
  12.8 0.1 multiply_reduce_fusion.1
  13.0 0.2 convert_reduce_fusion
  13.2 0.1 pad_add_fusion.1.meta
  13.3 0.2 select_reduce_fusion
  13.4 0.1 select_reduce_fusion.1.entries
  13.6 51.3 %all-gather.2.cloned.1.call-done.q_ref.kn_ref.vn_ref = bf16[1024,1024]{1,0:T(8,128)(2,1)} async-done(((bf16[128,1024]{1,0:T(8,128)(2,1)}), bf16[1024,1024]{1,0:T(8,128)(2,1)}) %all-gather.2.cloned.1.call-update) | async-done | bytes 2097168 | tf_op jit(solution)/shard_map/all_gather | solution.py:223
  64.9 1.6 copy-done.1
  66.5 29.4 %shard_map.118 = (bf16[4,1024,128]{2,1,0:T(8,128)(2,1)S(1)}, f32[2,4,512]{2,1,0:T(4,128)}) custom-call(s32[2,64]{1,0:T(2,128)S(1)} %select_reduce_fusion.1.entries, s32[2]{0:T(128)S(1)} %get-tuple-element.11.counts, s32[2]{0:T(128)S(1)} %pad_add_fusion.1.meta, bf16[1024,1024]{1,0:T(8,128)(2,1)S(1)} %copy-done.1, bf16[1024,1024]{1,0:T(8,128)(2,1)S(1)} %copy-done.1, ...), custom_call_target="tpu_custom_call" | custom-call | flops 8589934592 | bytes 8388608 | tf_op jit(solution)/shard_map/pallas_call | solution.py:126
  95.9 3.3 %all-to-all-start.1 = ((f32[4,8,128]{2,0,1:T(4,128)}), f32[4,8,128]{2,0,1:T(4,128)S(1)}, u32[]{:S(2)}, u32[]{:S(2)}) async-start(f32[4,8,128]{2,0,1:T(4,128)} %bitcast.4), calls=%async_computation.1 | async-start | bytes 32768 | tf_op jit(solution)/shard_map/all_to_all | solution.py:241
  99.2 1.1 copy.19
  100.3 5.4 %all-to-all-done.1 = f32[4,8,128]{2,0,1:T(4,128)S(1)} async-done(((f32[4,8,128]{2,0,1:T(4,128)}), f32[4,8,128]{2,0,1:T(4,128)S(1)}, u32[]{:S(2)}, u32[]{:S(2)}) %all-to-all-start.1) | async-done | bytes 16416 | tf_op jit(solution)/shard_map/all_to_all | solution.py:241
  105.7 3.6 %all-to-all-start = ((bf16[4,8,128,128]{3,2,0,1:T(8,128)(2,1)}), bf16[4,8,128,128]{3,2,0,1:T(8,128)(2,1)S(1)}, u32[]{:S(2)}, u32[]{:S(2)}) async-start(bf16[4,8,128,128]{3,2,0,1:T(8,128)(2,1)} %copy.19), calls=%async_computation | async-start | bytes 2097152 | tf_op jit(solution)/shard_map/all_to_all | solution.py:234
  109.3 0.0 reduce-scatter.2.cloned.1.call-start
  109.4 24.4 %all-to-all-done = bf16[4,8,128,128]{3,2,0,1:T(8,128)(2,1)S(1)} async-done(((bf16[4,8,128,128]{3,2,0,1:T(8,128)(2,1)}), bf16[4,8,128,128]{3,2,0,1:T(8,128)(2,1)S(1)}, u32[]{:S(2)}, u32[]{:S(2)}) %all-to-all-start) | async-done | bytes 1048608 | tf_op jit(solution)/shard_map/all_to_all | solution.py:234
  133.7 0.7 multiply_reduce_fusion
  134.5 0.1 fusion.3
  134.6 0.1 copy.23
  134.8 1.5 fusion.9
  136.2 0.0 reduce-scatter.2.cloned.1.call-update
  136.2 23.9 %reduce-scatter.2.cloned.1.call-done = f32[128,512]{1,0:T(8,128)} async-done(((f32[128,2048]{1,0:T(8,128)}), f32[128,512]{1,0:T(8,128)}) %reduce-scatter.2.cloned.1.call-update) | async-done | bytes 262160 | tf_op jit(solution)/shard_map/reduce_scatter | solution.py:258
  160.1 1.6 convert_element_type.51
  (22 shorter events, 0.1 us)
Async XLA Ops:
  6.5 128.2 %copy-start = (bf16[512,2048]{1,0:T(8,128)(2,1)S(1)}, bf16[512,2048]{1,0:T(8,128)(2,1)}, u32[]{:S(2)}) copy-start(bf16[512,2048]{1,0:T(8,128)(2,1)} %param.17) | copy-start | bytes 6291460
  6.5 3.2 %copy-start.2 = (bf16[128,2048]{1,0:T(8,128)(2,1)S(1)}, bf16[128,2048]{1,0:T(8,128)(2,1)}, u32[]{:S(2)}) copy-start(bf16[128,2048]{1,0:T(8,128)(2,1)} %param.12) | copy-start | bytes 1572868
  6.5 3.2 %copy-start.6 = (f32[2048]{0:T(1024)S(1)}, f32[2048]{0:T(1024)}, u32[]{:S(2)}) copy-start(f32[2048]{0:T(1024)} %param.13) | copy-start | bytes 24580
  6.5 58.3 %all-gather.2.cloned.1.call-start = ((), (), s32[]{:S(2)}) async-start(), calls=%async_computation.3 | async-start | bytes 2359296 | tf_op jit(solution)/shard_map/all_gather | solution.py:223
  6.5 4.8 %copy-start.5 = (bf16[2048,512]{1,0:T(8,128)(2,1)S(1)}, bf16[2048,512]{1,0:T(8,128)(2,1)}, u32[]{:S(2)}) copy-start(bf16[2048,512]{1,0:T(8,128)(2,1)} %param.14) | copy-start | bytes 6291460
  11.4 1.4 copy-start.7
  11.4 1.4 copy-start.3
  11.4 1.5 copy-start.8
  11.4 1.5 copy-start.4
  64.9 1.6 copy-start.1
  95.9 9.9 %all-to-all-start.1 = ((f32[4,8,128]{2,0,1:T(4,128)}), f32[4,8,128]{2,0,1:T(4,128)S(1)}, u32[]{:S(2)}, u32[]{:S(2)}) async-start(f32[4,8,128]{2,0,1:T(4,128)} %bitcast.4), calls=%async_computation.1 | async-start | bytes 32768 | tf_op jit(solution)/shard_map/all_to_all | solution.py:241
  105.7 28.0 %all-to-all-start = ((bf16[4,8,128,128]{3,2,0,1:T(8,128)(2,1)}), bf16[4,8,128,128]{3,2,0,1:T(8,128)(2,1)S(1)}, u32[]{:S(2)}, u32[]{:S(2)}) async-start(bf16[4,8,128,128]{3,2,0,1:T(8,128)(2,1)} %copy.19), calls=%async_computation | async-start | bytes 2097152 | tf_op jit(solution)/shard_map/all_to_all | solution.py:234
  109.3 50.8 %reduce-scatter.2.cloned.1.call-start = ((), (), s32[]{:S(2)}) async-start(), calls=%async_computation.4 | async-start | bytes 1310720 | tf_op jit(solution)/shard_map/reduce_scatter | solution.py:258
Sparse Core Ops, SparseCore 0:
  12.8 51.9 all-gather.1
  136.4 23.7 reduce-scatter.1

commit v2 on v1

--- a/solution.py
+++ b/solution.py
@@ -18,6 +18,8 @@
 SCORE_SCALE = 1.0 / math.sqrt(HEAD_DIM)
 EXP2_SCALE = SCORE_SCALE * math.log2(math.e)
 EMPTY = -1e30
+LINES = 8
+MESH = pl.DeviceIdType.MESH
 
 
 def dot_nt(left, right):
@@ -43,8 +45,9 @@
     acc_ref,
 ):
     request = pl.program_id(0)
-    heads = o_ref.shape[0]
+    heads = m_ref.shape[0]
     kv_count = heads // per_kv
+    ls_ref[...] = jnp.zeros_like(ls_ref)
     m_ref[...] = jnp.full_like(m_ref, EMPTY)
     acc_ref[...] = jnp.zeros_like(acc_ref)
 
@@ -104,17 +107,19 @@
     )
     for head in range(heads):
         den = jnp.maximum(acc_ref[head, :, HEAD_DIM:], 1.0)
-        o_ref[head] = (acc_ref[head, :, :HEAD_DIM] / den).astype(jnp.bfloat16)
+        o_ref[:, cols(head)] = (acc_ref[head, :, :HEAD_DIM] / den).astype(jnp.bfloat16)
         scale = m_ref[head] * SCORE_SCALE + jnp.log(den)
         for block in range(ADDED_TOKENS // 128):
             part = scale[block * 128 : (block + 1) * 128]
-            ls_ref[0, head : head + 1, block * 128 : (block + 1) * 128] = jnp.sum(
-                jnp.where(eye, part, 0.0), axis=0, keepdims=True
-            )
-
-
-def attend(entries, counts, meta, gathered, key_cache, value_cache, per_kv, tok_rows):
-    total_rows = gathered.shape[0]
+            line = jnp.sum(jnp.where(eye, part, 0.0), axis=0, keepdims=True)
+            for piece in range(128 // tok_rows):
+                ls_ref[block * (128 // tok_rows) + piece, head : head + 1, :] = line[
+                    :, piece * tok_rows : (piece + 1) * tok_rows
+                ]
+
+
+def attend(entries, counts, meta, queries, fresh, key_cache, value_cache, per_kv, tok_rows):
+    total_rows = queries.shape[0]
     requests = total_rows // ADDED_TOKENS
     kv_cols = key_cache.shape[2]
     heads = kv_cols // HEAD_DIM * per_kv
@@ -126,24 +131,24 @@
     return pl.pallas_call(
         functools.partial(attend_kernel, per_kv, tok_rows),
         out_shape=(
-            jax.ShapeDtypeStruct((heads, total_rows, HEAD_DIM), jnp.bfloat16),
-            jax.ShapeDtypeStruct((requests, heads, ADDED_TOKENS), jnp.float32),
+            jax.ShapeDtypeStruct((total_rows, q_cols), jnp.bfloat16),
+            jax.ShapeDtypeStruct((total_rows // tok_rows, LINES, tok_rows), jnp.float32),
         ),
         grid_spec=pltpu.PrefetchScalarGridSpec(
             num_scalar_prefetch=3,
             grid=(requests,),
             in_specs=[
                 pl.BlockSpec((ADDED_TOKENS, q_cols), lambda r, e, c, m: (r, 0)),
-                pl.BlockSpec((ADDED_TOKENS, kv_cols), lambda r, e, c, m: (m[0], q_cols // kv_cols)),
-                pl.BlockSpec(
-                    (ADDED_TOKENS, kv_cols), lambda r, e, c, m: (m[0], q_cols // kv_cols + 1)
-                ),
+                pl.BlockSpec((ADDED_TOKENS, kv_cols), lambda r, e, c, m: (0, 0)),
+                pl.BlockSpec((ADDED_TOKENS, kv_cols), lambda r, e, c, m: (0, 1)),
                 whole,
                 whole,
             ],
             out_specs=(
-                pl.BlockSpec((heads, ADDED_TOKENS, HEAD_DIM), lambda r, e, c, m: (0, r, 0)),
-                pl.BlockSpec((1, heads, ADDED_TOKENS), lambda r, e, c, m: (r, 0, 0)),
+                pl.BlockSpec((ADDED_TOKENS, q_cols), lambda r, e, c, m: (r, 0)),
+                pl.BlockSpec(
+                    (ADDED_TOKENS // tok_rows, LINES, tok_rows), lambda r, e, c, m: (r, 0, 0)
+                ),
             ),
             scratch_shapes=[
                 pltpu.VMEM((heads, ADDED_TOKENS, HEAD_DIM), jnp.float32),
@@ -158,7 +163,7 @@
             bytes_accessed=4 * pages * PAGE_ROWS * kv_cols,
             transcendentals=pages * PAGE_ROWS * ADDED_TOKENS * heads,
         ),
-    )(entries, counts, meta, gathered, gathered, gathered, key_cache, value_cache)
+    )(entries, counts, meta, queries, fresh, fresh, key_cache, value_cache)
 
 
 def page_lists(cached_lengths, group_ids, prompt_pages, own_pages, pages_dev, seq_index):
@@ -190,6 +195,323 @@
         axis=2,
     )
     return entries, jnp.sum(marks, axis=1)
+
+
+def greet(peers):
+    barrier = pltpu.get_barrier_semaphore()
+    for peer in peers:
+        pl.semaphore_signal(barrier, inc=1, device_id=peer, device_id_type=MESH)
+    pl.semaphore_wait(barrier, len(peers))
+
+
+def remote(source, target, send_sem, recv_sem, peer):
+    return pltpu.make_async_remote_copy(
+        src_ref=source,
+        dst_ref=target,
+        send_sem=send_sem,
+        recv_sem=recv_sem,
+        device_id=peer,
+        device_id_type=MESH,
+    )
+
+
+def gather_kernel(
+    seq_count,
+    x_ref,
+    gain_ref,
+    wq_ref,
+    wk_ref,
+    wv_ref,
+    q_ref,
+    kv_ref,
+    q_send,
+    q_recv,
+    qy_send,
+    qy_recv,
+    kv_send,
+    kv_recv,
+    kvy_send,
+    kvy_recv,
+):
+    tok_rows = x_ref.shape[0]
+    kv_cols = wk_ref.shape[1]
+    me = lax.axis_index("seq")
+    tensor = lax.axis_index("tensor")
+    outer = seq_count // 2
+    span = outer * ADDED_TOKENS // q_ref.shape[0]
+    place, side = me // 2, me % 2
+    base, inside = (place // span) * span, place % span
+    twin = (place * 2 + 1 - side, tensor)
+
+    def line_peer(distance):
+        return (place + distance) % outer * 2 + side
+
+    def span_peer(distance):
+        return (base + (inside + distance) % span) * 2 + side
+
+    def q_rows(owner):
+        return pl.ds(pl.multiple_of(owner * tok_rows, tok_rows), tok_rows)
+
+    def kv_rows(owner):
+        local = owner - base * 2
+        return pl.ds(pl.multiple_of(local * tok_rows, tok_rows), tok_rows)
+
+    greet([twin] + [(line_peer(distance), tensor) for distance in range(1, outer)])
+
+    floats = x_ref[...].astype(jnp.float32)
+    mean = jnp.mean(floats * floats, axis=-1, keepdims=True)
+    normed = (floats * lax.rsqrt(mean + 1e-05) * gain_ref[...]).astype(jnp.bfloat16)
+
+    mine = q_rows(me)
+    q_ref[mine, :] = jnp.dot(normed, wq_ref[...], preferred_element_type=jnp.float32).astype(
+        jnp.bfloat16
+    )
+    started = []
+    own = q_ref.at[mine, :]
+    for distance in range(1, outer):
+        peer = (line_peer(distance), tensor)
+        copy = remote(own, own, q_send.at[distance], q_recv.at[distance], peer)
+        copy.start()
+        started.append(copy)
+    copy = remote(own, own, qy_send.at[0], qy_recv.at[0], twin)
+    copy.start()
+    started.append(copy)
+
+    mine = kv_rows(me)
+    for start, weight in ((0, wk_ref), (kv_cols, wv_ref)):
+        kv_ref[mine, start : start + kv_cols] = jnp.dot(
+            normed, weight[...], preferred_element_type=jnp.float32
+        ).astype(jnp.bfloat16)
+    own = kv_ref.at[mine, :]
+    for distance in range(1, span):
+        peer = (span_peer(distance), tensor)
+        copy = remote(own, own, kv_send.at[distance], kv_recv.at[distance], peer)
+        copy.start()
+        started.append(copy)
+    copy = remote(own, own, kvy_send.at[0], kvy_recv.at[0], twin)
+    copy.start()
+    started.append(copy)
+
+    late = []
+    for distance in range(1, outer):
+        owner = line_peer(outer - distance)
+        block = q_ref.at[q_rows(owner), :]
+        remote(block, block, q_send.at[distance], q_recv.at[distance], twin).wait_recv()
+        copy = remote(block, block, qy_send.at[distance], qy_recv.at[distance], twin)
+        copy.start()
+        started.append(copy)
+        if distance < span:
+            owner = span_peer(span - distance)
+            block = kv_ref.at[kv_rows(owner), :]
+            remote(block, block, kv_send.at[distance], kv_recv.at[distance], twin).wait_recv()
+            copy = remote(block, block, kvy_send.at[distance], kvy_recv.at[distance], twin)
+            copy.start()
+            started.append(copy)
+    for distance in range(outer):
+        owner = (place + outer - distance) % outer * 2 + 1 - side
+        block = q_ref.at[q_rows(owner), :]
+        late.append(remote(block, block, qy_send.at[distance], qy_recv.at[distance], twin))
+    for distance in range(span):
+        owner = (base + (inside + span - distance) % span) * 2 + 1 - side
+        block = kv_ref.at[kv_rows(owner), :]
+        late.append(remote(block, block, kvy_send.at[distance], kvy_recv.at[distance], twin))
+    for copy in late:
+        copy.wait_recv()
+    for copy in started:
+        copy.wait_send()
+
+
+def gather(hidden_in, norm_gain, query_weight, key_weight, value_weight, seq_count):
+    tok_rows = hidden_in.shape[0]
+    q_cols, kv_cols = query_weight.shape[1], key_weight.shape[1]
+    slots = pltpu.SemaphoreType.DMA((seq_count // 2,))
+    vmem = pl.BlockSpec(memory_space=pltpu.VMEM)
+    return pl.pallas_call(
+        functools.partial(gather_kernel, seq_count),
+        out_shape=(
+            jax.ShapeDtypeStruct((tok_rows * seq_count, q_cols), jnp.bfloat16),
+            jax.ShapeDtypeStruct((ADDED_TOKENS, 2 * kv_cols), jnp.bfloat16),
+        ),
+        in_specs=[vmem] * 5,
+        out_specs=(vmem, vmem),
+        scratch_shapes=[slots] * 8,
+        compiler_params=pltpu.CompilerParams(
+            collective_id=0, has_side_effects=True, vmem_limit_bytes=24 << 20
+        ),
+    )(hidden_in, norm_gain.reshape(1, -1), query_weight, key_weight, value_weight)
+
+
+def finish_kernel(
+    seq_count,
+    tensor_count,
+    part_ref,
+    ls_ref,
+    w_ref,
+    out_ref,
+    got_ref,
+    gls_ref,
+    near_ref,
+    near_got,
+    far_ref,
+    far_got,
+    part_send,
+    part_recv,
+    ls_send,
+    ls_recv,
+    near_send,
+    near_recv,
+    far_send,
+    far_recv,
+):
+    tok_rows, out_cols = out_ref.shape
+    heads = part_ref.shape[1] // HEAD_DIM
+    me = lax.axis_index("seq")
+    tensor = lax.axis_index("tensor")
+    pair, core = tensor // 2, tensor % 2
+    pairs = tensor_count // 2
+    twin = (me, pair * 2 + 1 - core)
+
+    def far_pair(distance):
+        return (pair + distance) % pairs
+
+    def seq_peer(distance):
+        return (me + distance) % seq_count
+
+    greet(
+        [(seq_peer(distance), tensor) for distance in range(1, seq_count)]
+        + [twin]
+        + [(me, far_pair(distance) * 2 + core) for distance in range(1, pairs)]
+    )
+    scales, parts = [], []
+    for distance in range(1, seq_count):
+        owner = seq_peer(distance)
+        copy = remote(
+            ls_ref.at[owner],
+            gls_ref.at[distance],
+            ls_send.at[distance],
+            ls_recv.at[distance],
+            (owner, tensor),
+        )
+        copy.start()
+        scales.append(copy)
+    for distance in range(1, seq_count):
+        owner = seq_peer(distance)
+        copy = remote(
+            part_ref.at[pl.ds(pl.multiple_of(owner * tok_rows, tok_rows), tok_rows), :],
+            got_ref.at[distance],
+            part_send.at[distance],
+            part_recv.at[distance],
+            (owner, tensor),
+        )
+        copy.start()
+        parts.append(copy)
+    gls_ref[0] = ls_ref[me]
+    for copy in scales:
+        copy.wait_recv()
+    lines = gls_ref[...]
+    lines = jnp.exp(lines - jnp.max(lines, axis=0, keepdims=True))
+    lines = lines / jnp.sum(lines, axis=0, keepdims=True)
+    eye = (
+        lax.broadcasted_iota(jnp.int32, (tok_rows, tok_rows), 0)
+        == lax.broadcasted_iota(jnp.int32, (tok_rows, tok_rows), 1)
+    ).astype(jnp.float32)
+    shares = lax.dot_general(
+        eye,
+        lines.reshape(seq_count * LINES, tok_rows),
+        (((1,), (1,)), ((), ())),
+        precision=lax.Precision.HIGHEST,
+        preferred_element_type=jnp.float32,
+    )
+
+    def weighted(block, distance):
+        return [
+            block[:, head * HEAD_DIM : (head + 1) * HEAD_DIM].astype(jnp.float32)
+            * shares[:, distance * LINES + head : distance * LINES + head + 1]
+            for head in range(heads)
+        ]
+
+    mine = pl.ds(pl.multiple_of(me * tok_rows, tok_rows), tok_rows)
+    total = weighted(part_ref[mine, :], 0)
+    for distance in range(1, seq_count):
+        parts[distance - 1].wait_recv()
+        terms = weighted(got_ref[distance], distance)
+        total = [left + right for left, right in zip(total, terms)]
+    attention = jnp.concatenate(total, axis=1).astype(jnp.bfloat16)
+
+    def terms_for(owner):
+        start = pl.multiple_of(owner * out_cols, out_cols)
+        return jnp.dot(
+            attention, w_ref[:, pl.ds(start, out_cols)], preferred_element_type=jnp.float32
+        )
+
+    started = []
+    nears = []
+    for distance in list(range(1, pairs)) + [0]:
+        near_ref[distance] = terms_for(far_pair(distance) * 2 + 1 - core)
+        copy = remote(
+            near_ref.at[distance],
+            near_got.at[distance],
+            near_send.at[distance],
+            near_recv.at[distance],
+            twin,
+        )
+        copy.start()
+        started.append(copy)
+        nears.append((distance, copy))
+    fars = []
+    for distance, copy in nears[:-1]:
+        owner = far_pair(distance) * 2 + core
+        terms = terms_for(owner)
+        copy.wait_recv()
+        far_ref[distance] = terms + near_got[distance]
+        copy = remote(
+            far_ref.at[distance],
+            far_got.at[distance],
+            far_send.at[distance],
+            far_recv.at[distance],
+            (me, owner),
+        )
+        copy.start()
+        started.append(copy)
+        fars.append(copy)
+    result = terms_for(tensor)
+    nears[-1][1].wait_recv()
+    result = result + near_got[0]
+    for distance in range(1, pairs):
+        fars[distance - 1].wait_recv()
+        result = result + far_got[distance]
+    out_ref[...] = result.astype(jnp.bfloat16)
+    for copy in scales + parts + started:
+        copy.wait_send()
+
+
+def finish(partial_value, log_scale, out_weight, seq_count, tensor_count):
+    tok_rows = partial_value.shape[0] // seq_count
+    out_cols = out_weight.shape[1] // tensor_count
+    pairs = tensor_count // 2
+    vmem = pl.BlockSpec(memory_space=pltpu.VMEM)
+    block = pltpu.VMEM((pairs, tok_rows, out_cols), jnp.float32)
+    seq_sems = pltpu.SemaphoreType.DMA((seq_count,))
+    pair_sems = pltpu.SemaphoreType.DMA((pairs,))
+    return pl.pallas_call(
+        functools.partial(finish_kernel, seq_count, tensor_count),
+        out_shape=jax.ShapeDtypeStruct((tok_rows, out_cols), jnp.bfloat16),
+        in_specs=[vmem] * 3,
+        out_specs=vmem,
+        scratch_shapes=[
+            pltpu.VMEM((seq_count, tok_rows, partial_value.shape[1]), jnp.bfloat16),
+            pltpu.VMEM((seq_count, LINES, tok_rows), jnp.float32),
+            block,
+            block,
+            block,
+            block,
+        ]
+        + [seq_sems] * 4
+        + [pair_sems] * 4,
+        compiler_params=pltpu.CompilerParams(
+            collective_id=1, has_side_effects=True, vmem_limit_bytes=24 << 20
+        ),
+    )(partial_value, log_scale, out_weight)
 
 
 def body(
@@ -212,15 +534,9 @@
     heads_dev = query_weight.shape[1] // HEAD_DIM
     kv_dev = key_weight.shape[1] // HEAD_DIM
     per_kv = heads_dev // kv_dev
-    floats = hidden_in.astype(jnp.float32)
-    normed = (
-        floats * lax.rsqrt(jnp.mean(floats * floats, axis=-1, keepdims=True) + 1e-05) * norm_gain
-    ).astype(jnp.bfloat16)
-    projected = [
-        jnp.dot(normed, weight, preferred_element_type=jnp.float32).astype(jnp.bfloat16)
-        for weight in (query_weight, key_weight, value_weight)
-    ]
-    gathered = lax.all_gather(jnp.concatenate(projected, axis=1), "seq", axis=0, tiled=True)
+    queries, fresh = gather(
+        hidden_in, norm_gain, query_weight, key_weight, value_weight, seq_count
+    )
     entries, counts = page_lists(
         cached_lengths, group_ids, prompt_pages, own_pages, key_cache.shape[0], seq_index
     )
@@ -228,36 +544,9 @@
     home = my_start // ADDED_TOKENS
     meta = jnp.stack([home, my_start - home * ADDED_TOKENS]).astype(jnp.int32)
     partial_value, log_scale = attend(
-        entries, counts, meta, gathered, key_cache, value_cache, per_kv, tok_rows
-    )
-    log_scale = log_scale.transpose(1, 0, 2)
-    got_part = lax.all_to_all(
-        partial_value.reshape(heads_dev, seq_count, tok_rows, HEAD_DIM),
-        "seq",
-        split_axis=1,
-        concat_axis=1,
-        tiled=True,
-    )
-    got_scale = lax.all_to_all(
-        log_scale.reshape(heads_dev, seq_count, tok_rows),
-        "seq",
-        split_axis=1,
-        concat_axis=1,
-        tiled=True,
-    )
-    highest = jnp.max(got_scale, axis=1)
-    scale_weights = jnp.exp(got_scale - highest[:, None])
-    attention = (
-        jnp.sum(got_part.astype(jnp.float32) * scale_weights[..., None], axis=1)
-        / jnp.sum(scale_weights, axis=1)[..., None]
-    )
-    attention = (
-        attention.transpose(1, 0, 2).reshape(tok_rows, heads_dev * HEAD_DIM).astype(jnp.bfloat16)
-    )
-    head_terms = jnp.dot(attention, out_weight, preferred_element_type=jnp.float32)
-    return lax.psum_scatter(head_terms, "tensor", scatter_dimension=1, tiled=True).astype(
-        jnp.bfloat16
-    )
+        entries, counts, meta, queries, fresh, key_cache, value_cache, per_kv, tok_rows
+    )
+    return finish(partial_value, log_scale, out_weight, seq_count, lax.axis_size("tensor"))
 
 
 def solution(mesh):

time: 171 us -> 107 us (0.63)
  the two profiles are of different devices: /device:TPU:0 before, /device:TPU:13 now
where the time goes in v2:
time: 107 us; the launch traced here: 109 us
  Pallas kernels  99.4 us (93%)
  local copies, waits for them, and re-layouts  6.44 us (6%)
  other arithmetic  3.41 us (3%)
    pallas_call x1, Pallas kernels, finish(): pl.pallas_call(functools.partial(finish_kernel, seq_count, tensor_count),...  46.9 us
    pallas_call x1, Pallas kernels, attend(): pl.pallas_call(functools.partial(attend_kernel, per_kv, tok_rows), out_sh...  28.7 us
    pallas_call x1, Pallas kernels, gather(): pl.pallas_call(functools.partial(gather_kernel, seq_count), out_shape=(ja...  23.8 us
    unnamed x13, local copies, waits for them, and re-layouts  6.44 us

profile of v2, /device:TPU:13, one launch (start us, length us, event | category | flops | bytes accessed | tf_op | source)
XLA Modules:
  0.0 109.3 jit_solution(243938055437230890)
XLA Ops:
  0.0 0.1 pad_add_fusion.1.meta
  0.1 0.7 broadcast_add_fusion
  0.7 0.7 compare_convert_fusion
  1.5 0.8 multiply_reduce_fusion
  2.2 0.9 convert_reduce_fusion
  3.1 0.2 select_reduce_fusion
  3.3 0.1 select_reduce_fusion.1.entries
  3.4 0.0 copy-start
  3.4 1.6 %copy-done = bf16[2048,512]{1,0:T(8,128)(2,1)S(1)} copy-done((bf16[2048,512]{1,0:T(8,128)(2,1)S(1)}, bf16[2048,512]{1,0:T(8,128)(2,1)}, u32[]{:S(2)}) %copy-start) | copy-done | bytes 2097176
  5.0 0.0 copy-start.2
  5.0 1.2 %copy-done.2 = bf16[2048,256]{1,0:T(8,128)(2,1)S(1)} copy-done((bf16[2048,256]{1,0:T(8,128)(2,1)S(1)}, bf16[2048,256]{1,0:T(8,128)(2,1)}, u32[]{:S(2)}) %copy-start.2) | copy-done | bytes 1048600
  6.2 0.0 copy-start.3
  6.3 1.2 %copy-done.3 = bf16[2048,256]{1,0:T(8,128)(2,1)S(1)} copy-done((bf16[2048,256]{1,0:T(8,128)(2,1)S(1)}, bf16[2048,256]{1,0:T(8,128)(2,1)}, u32[]{:S(2)}) %copy-start.3) | copy-done | bytes 1048600
  7.5 0.0 copy-start.4
  7.5 1.0 copy-done.4
  8.5 0.0 copy-start.5
  8.5 0.7 copy-done.5
  9.2 23.8 %shard_map.118 = (bf16[1024,512]{1,0:T(8,128)(2,1)S(1)}, bf16[512,512]{1,0:T(8,128)(2,1)S(1)}) custom-call(bf16[128,2048]{1,0:T(8,128)(2,1)S(1)} %copy-done.4, f32[1,2048]{1,0:T(1,128)S(1)} %bitcast.3, bf16[2048,512]{1,0:T(8,128)(2,1)S(1)} %copy-done, bf16[2048,256]{1,0:T(8,128)(2,1)S(1)} %copy-done.2, bf16[2048,256]{1,0:T(8,128)(2,1)S(1)} %copy-done.3), custom_call_target="tpu_custom_call" | custom-call | tf_op jit(solution)/shard_map/pallas_call | solution.py:329
  33.1 0.0 copy-start.1
  33.1 28.7 %shard_map.119 = (bf16[1024,512]{1,0:T(8,128)(2,1)S(1)}, f32[8,8,128]{2,1,0:T(8,128)S(1)}) custom-call(s32[2,64]{1,0:T(2,128)S(1)} %select_reduce_fusion.1.entries, s32[2]{0:T(128)S(1)} %get-tuple-element.13.counts, s32[2]{0:T(128)S(1)} %pad_add_fusion.1.meta, bf16[1024,512]{1,0:T(8,128)(2,1)S(1)} %get-tuple-element.9.q_ref, ...), custom_call_target="tpu_custom_call" | custom-call | flops 8589934592 | bytes 8388608 | tf_op jit(solution)/shard_map/pallas_call | solution.py:131
  61.8 0.0 copy-done.1
  61.8 46.9 %shard_map.120 = bf16[128,512]{1,0:T(8,128)(2,1)S(1)} custom-call(bf16[1024,512]{1,0:T(8,128)(2,1)S(1)} %get-tuple-element.11.part_ref, f32[8,8,128]{2,1,0:T(8,128)S(1)} %get-tuple-element.12.ls_ref, bf16[512,2048]{1,0:T(8,128)(2,1)S(1)} %copy-done.1), custom_call_target="tpu_custom_call" | custom-call | tf_op jit(solution)/shard_map/pallas_call | solution.py:496
  108.7 0.7 copy.14
  (4 shorter events, 0.0 us)
Async XLA Ops:
  3.4 1.6 %copy-start = (bf16[2048,512]{1,0:T(8,128)(2,1)S(1)}, bf16[2048,512]{1,0:T(8,128)(2,1)}, u32[]{:S(2)}) copy-start(bf16[2048,512]{1,0:T(8,128)(2,1)} %wq_ref.1) | copy-start | bytes 6291460
  5.0 1.2 %copy-start.2 = (bf16[2048,256]{1,0:T(8,128)(2,1)S(1)}, bf16[2048,256]{1,0:T(8,128)(2,1)}, u32[]{:S(2)}) copy-start(bf16[2048,256]{1,0:T(8,128)(2,1)} %wk_ref.1) | copy-start | bytes 3145732
  6.2 1.2 %copy-start.3 = (bf16[2048,256]{1,0:T(8,128)(2,1)S(1)}, bf16[2048,256]{1,0:T(8,128)(2,1)}, u32[]{:S(2)}) copy-start(bf16[2048,256]{1,0:T(8,128)(2,1)} %wv_ref.1) | copy-start | bytes 3145732
  7.5 1.0 copy-start.4
  8.5 0.7 copy-start.5
  33.1 28.7 %copy-start.1 = (bf16[512,2048]{1,0:T(8,128)(2,1)S(1)}, bf16[512,2048]{1,0:T(8,128)(2,1)}, u32[]{:S(2)}) copy-start(bf16[512,2048]{1,0:T(8,128)(2,1)} %w_ref.1) | copy-start | bytes 6291460

commit v3 on v2

--- a/solution.py
+++ b/solution.py
@@ -232,9 +232,21 @@
     kv_recv,
     kvy_send,
     kvy_recv,
+    wq_buf,
+    wk_buf,
+    wv_buf,
+    load_sem,
 ):
     tok_rows = x_ref.shape[0]
     kv_cols = wk_ref.shape[1]
+    loads = [
+        pltpu.make_async_copy(source, target, load_sem.at[index])
+        for index, (source, target) in enumerate(
+            ((wq_ref, wq_buf), (wk_ref, wk_buf), (wv_ref, wv_buf))
+        )
+    ]
+    for load in loads:
+        load.start()
     me = lax.axis_index("seq")
     tensor = lax.axis_index("tensor")
     outer = seq_count // 2
@@ -263,7 +275,8 @@
     normed = (floats * lax.rsqrt(mean + 1e-05) * gain_ref[...]).astype(jnp.bfloat16)
 
     mine = q_rows(me)
-    q_ref[mine, :] = jnp.dot(normed, wq_ref[...], preferred_element_type=jnp.float32).astype(
+    loads[0].wait()
+    q_ref[mine, :] = jnp.dot(normed, wq_buf[...], preferred_element_type=jnp.float32).astype(
         jnp.bfloat16
     )
     started = []
@@ -278,7 +291,9 @@
     started.append(copy)
 
     mine = kv_rows(me)
-    for start, weight in ((0, wk_ref), (kv_cols, wv_ref)):
+    loads[1].wait()
+    loads[2].wait()
+    for start, weight in ((0, wk_buf), (kv_cols, wv_buf)):
         kv_ref[mine, start : start + kv_cols] = jnp.dot(
             normed, weight[...], preferred_element_type=jnp.float32
         ).astype(jnp.bfloat16)
@@ -332,9 +347,14 @@
             jax.ShapeDtypeStruct((tok_rows * seq_count, q_cols), jnp.bfloat16),
             jax.ShapeDtypeStruct((ADDED_TOKENS, 2 * kv_cols), jnp.bfloat16),
         ),
-        in_specs=[vmem] * 5,
+        in_specs=[vmem] * 2 + [pl.BlockSpec(memory_space=pltpu.HBM)] * 3,
         out_specs=(vmem, vmem),
-        scratch_shapes=[slots] * 8,
+        scratch_shapes=[slots] * 8
+        + [
+            pltpu.VMEM(weight.shape, weight.dtype)
+            for weight in (query_weight, key_weight, value_weight)
+        ]
+        + [pltpu.SemaphoreType.DMA((3,))],
         compiler_params=pltpu.CompilerParams(
             collective_id=0, has_side_effects=True, vmem_limit_bytes=24 << 20
         ),
@@ -348,16 +368,24 @@
     ls_ref,
     w_ref,
     out_ref,
-    got_ref,
+    mix_ref,
+    mix_got,
+    mls_ref,
+    side_got,
+    sls_ref,
     gls_ref,
     near_ref,
     near_got,
     far_ref,
     far_got,
-    part_send,
-    part_recv,
-    ls_send,
-    ls_recv,
+    side_send,
+    side_recv,
+    sls_send,
+    sls_recv,
+    mix_send,
+    mix_recv,
+    mls_send,
+    mls_recv,
     near_send,
     near_recv,
     far_send,
@@ -370,72 +398,121 @@
     pair, core = tensor // 2, tensor % 2
     pairs = tensor_count // 2
     twin = (me, pair * 2 + 1 - core)
+    outer = seq_count // 2
+    place, side = me // 2, me % 2
+    beside = (place * 2 + 1 - side, tensor)
+    order = sorted(range(1, outer), key=lambda distance: -min(distance, outer - distance))
 
     def far_pair(distance):
         return (pair + distance) % pairs
 
-    def seq_peer(distance):
-        return (me + distance) % seq_count
+    def line(distance, which):
+        return (place + distance) % outer * 2 + which
+
+    def rows(owner):
+        return pl.ds(pl.multiple_of(owner * tok_rows, tok_rows), tok_rows)
 
     greet(
-        [(seq_peer(distance), tensor) for distance in range(1, seq_count)]
+        [beside]
+        + [(line(distance, side), tensor) for distance in range(1, outer)]
         + [twin]
         + [(me, far_pair(distance) * 2 + core) for distance in range(1, pairs)]
     )
-    scales, parts = [], []
-    for distance in range(1, seq_count):
-        owner = seq_peer(distance)
-        copy = remote(
-            ls_ref.at[owner],
-            gls_ref.at[distance],
-            ls_send.at[distance],
-            ls_recv.at[distance],
-            (owner, tensor),
-        )
-        copy.start()
-        scales.append(copy)
-    for distance in range(1, seq_count):
-        owner = seq_peer(distance)
-        copy = remote(
-            part_ref.at[pl.ds(pl.multiple_of(owner * tok_rows, tok_rows), tok_rows), :],
-            got_ref.at[distance],
-            part_send.at[distance],
-            part_recv.at[distance],
-            (owner, tensor),
-        )
-        copy.start()
-        parts.append(copy)
-    gls_ref[0] = ls_ref[me]
-    for copy in scales:
-        copy.wait_recv()
-    lines = gls_ref[...]
-    lines = jnp.exp(lines - jnp.max(lines, axis=0, keepdims=True))
-    lines = lines / jnp.sum(lines, axis=0, keepdims=True)
+    started = []
+    scales, sides, mixes, mix_scales = {}, {}, {}, {}
+    for distance in order + [0]:
+        scales[distance] = remote(
+            ls_ref.at[line(distance, 1 - side)],
+            sls_ref.at[distance],
+            sls_send.at[distance],
+            sls_recv.at[distance],
+            beside,
+        )
+        scales[distance].start()
+    for distance in order + [0]:
+        sides[distance] = remote(
+            part_ref.at[rows(line(distance, 1 - side)), :],
+            side_got.at[distance],
+            side_send.at[distance],
+            side_recv.at[distance],
+            beside,
+        )
+        sides[distance].start()
+    for distance in order + [0]:
+        scales[distance].wait_recv()
     eye = (
         lax.broadcasted_iota(jnp.int32, (tok_rows, tok_rows), 0)
         == lax.broadcasted_iota(jnp.int32, (tok_rows, tok_rows), 1)
     ).astype(jnp.float32)
-    shares = lax.dot_general(
-        eye,
-        lines.reshape(seq_count * LINES, tok_rows),
-        (((1,), (1,)), ((), ())),
-        precision=lax.Precision.HIGHEST,
-        preferred_element_type=jnp.float32,
-    )
-
-    def weighted(block, distance):
+
+    def columns(lines):
+        return lax.dot_general(
+            eye,
+            lines.reshape(-1, tok_rows),
+            (((1,), (1,)), ((), ())),
+            precision=lax.Precision.HIGHEST,
+            preferred_element_type=jnp.float32,
+        )
+
+    def weighted(block, shares, index):
         return [
             block[:, head * HEAD_DIM : (head + 1) * HEAD_DIM].astype(jnp.float32)
-            * shares[:, distance * LINES + head : distance * LINES + head + 1]
+            * shares[:, index * LINES + head : index * LINES + head + 1]
             for head in range(heads)
         ]
 
-    mine = pl.ds(pl.multiple_of(me * tok_rows, tok_rows), tok_rows)
-    total = weighted(part_ref[mine, :], 0)
-    for distance in range(1, seq_count):
-        parts[distance - 1].wait_recv()
-        terms = weighted(got_ref[distance], distance)
-        total = [left + right for left, right in zip(total, terms)]
+    def plus(left, right):
+        return [one + other for one, other in zip(left, right)]
+
+    own_lines = jnp.stack([ls_ref[line(distance, side)] for distance in range(outer)])
+    side_lines = sls_ref[...]
+    top = jnp.maximum(own_lines, side_lines)
+    own_scale, side_scale = jnp.exp(own_lines - top), jnp.exp(side_lines - top)
+    both = own_scale + side_scale
+    mls_ref[...] = top + jnp.log(both)
+    for distance in order:
+        mix_scales[distance] = remote(
+            mls_ref.at[distance],
+            gls_ref.at[distance],
+            mls_send.at[distance],
+            mls_recv.at[distance],
+            (line(distance, side), tensor),
+        )
+        mix_scales[distance].start()
+    own_shares, side_shares = columns(own_scale / both), columns(side_scale / both)
+
+    def mixed(distance):
+        return plus(
+            weighted(part_ref[rows(line(distance, side)), :], own_shares, distance),
+            weighted(side_got[distance], side_shares, distance),
+        )
+
+    for distance in order:
+        sides[distance].wait_recv()
+        mix_ref[distance] = jnp.concatenate(mixed(distance), axis=1).astype(jnp.bfloat16)
+        mixes[distance] = remote(
+            mix_ref.at[distance],
+            mix_got.at[distance],
+            mix_send.at[distance],
+            mix_recv.at[distance],
+            (line(distance, side), tensor),
+        )
+        mixes[distance].start()
+    gls_ref[0] = mls_ref[0]
+    for distance in order:
+        mix_scales[distance].wait_recv()
+    lines = gls_ref[...]
+    lines = jnp.exp(lines - jnp.max(lines, axis=0, keepdims=True))
+    shares = columns(lines / jnp.sum(lines, axis=0, keepdims=True))
+    sides[0].wait_recv()
+    total = [
+        block * shares[:, head : head + 1] for head, block in enumerate(mixed(0))
+    ]
+    for distance in order:
+        mixes[distance].wait_recv()
+        total = plus(total, weighted(mix_got[distance], shares, distance))
+    for group in (scales, sides, mixes, mix_scales):
+        started.extend(group.values())
     attention = jnp.concatenate(total, axis=1).astype(jnp.bfloat16)
 
     def terms_for(owner):
@@ -444,7 +521,6 @@
             attention, w_ref[:, pl.ds(start, out_cols)], preferred_element_type=jnp.float32
         )
 
-    started = []
     nears = []
     for distance in list(range(1, pairs)) + [0]:
         near_ref[distance] = terms_for(far_pair(distance) * 2 + 1 - core)
@@ -481,7 +557,7 @@
         fars[distance - 1].wait_recv()
         result = result + far_got[distance]
     out_ref[...] = result.astype(jnp.bfloat16)
-    for copy in scales + parts + started:
+    for copy in started:
         copy.wait_send()
 
 
@@ -491,7 +567,10 @@
     pairs = tensor_count // 2
     vmem = pl.BlockSpec(memory_space=pltpu.VMEM)
     block = pltpu.VMEM((pairs, tok_rows, out_cols), jnp.float32)
-    seq_sems = pltpu.SemaphoreType.DMA((seq_count,))
+    outer = seq_count // 2
+    parts = pltpu.VMEM((outer, tok_rows, partial_value.shape[1]), jnp.bfloat16)
+    scales = pltpu.VMEM((outer, LINES, tok_rows), jnp.float32)
+    line_sems = pltpu.SemaphoreType.DMA((outer,))
     pair_sems = pltpu.SemaphoreType.DMA((pairs,))
     return pl.pallas_call(
         functools.partial(finish_kernel, seq_count, tensor_count),
@@ -499,14 +578,18 @@
         in_specs=[vmem] * 3,
         out_specs=vmem,
         scratch_shapes=[
-            pltpu.VMEM((seq_count, tok_rows, partial_value.shape[1]), jnp.bfloat16),
-            pltpu.VMEM((seq_count, LINES, tok_rows), jnp.float32),
+            parts,
+            parts,
+            scales,
+            parts,
+            scales,
+            scales,
             block,
             block,
             block,
             block,
         ]
-        + [seq_sems] * 4
+        + [line_sems] * 8
         + [pair_sems] * 4,
         compiler_params=pltpu.CompilerParams(
             collective_id=1, has_side_effects=True, vmem_limit_bytes=24 << 20

time: 107 us -> 96.4 us (0.901)
  the two profiles are of different devices: /device:TPU:13 before, /device:TPU:0 now
where the time goes in v3:
time: 96.4 us; the launch traced here: 98.1 us
  Pallas kernels  88.2 us (91%)
  local copies, waits for them, and re-layouts  6.44 us (7%)
  other arithmetic  3.41 us (4%)
    pallas_call x1, Pallas kernels, attend(): pl.pallas_call(functools.partial(attend_kernel, per_kv, tok_rows), out_sh...  31.9 us
    pallas_call x1, Pallas kernels, gather(): pl.pallas_call(functools.partial(gather_kernel, seq_count), out_shape=(ja...  29.3 us
    pallas_call x1, Pallas kernels, finish(): pl.pallas_call(functools.partial(finish_kernel, seq_count, tensor_count),...  27 us
    unnamed x13, local copies, waits for them, and re-layouts  6.44 us

profile of v3, /device:TPU:0, one launch (start us, length us, event | category | flops | bytes accessed | tf_op | source)
XLA Modules:
  0.0 98.1 jit_solution(10603289980382927698)
XLA Ops:
  0.0 0.1 pad_add_fusion.1.meta
  0.1 0.7 broadcast_add_fusion
  0.7 0.7 compare_convert_fusion
  1.5 0.8 multiply_reduce_fusion
  2.2 0.9 convert_reduce_fusion
  3.1 0.2 select_reduce_fusion
  3.3 0.1 select_reduce_fusion.1.entries
  3.4 0.0 copy-start
  3.4 1.6 %copy-done = bf16[2048,512]{1,0:T(8,128)(2,1)S(1)} copy-done((bf16[2048,512]{1,0:T(8,128)(2,1)S(1)}, bf16[2048,512]{1,0:T(8,128)(2,1)}, u32[]{:S(2)}) %copy-start) | copy-done | bytes 2097176
  5.0 0.0 copy-start.2
  5.0 1.2 %copy-done.2 = bf16[2048,256]{1,0:T(8,128)(2,1)S(1)} copy-done((bf16[2048,256]{1,0:T(8,128)(2,1)S(1)}, bf16[2048,256]{1,0:T(8,128)(2,1)}, u32[]{:S(2)}) %copy-start.2) | copy-done | bytes 1048600
  6.2 0.0 copy-start.3
  6.3 1.2 %copy-done.3 = bf16[2048,256]{1,0:T(8,128)(2,1)S(1)} copy-done((bf16[2048,256]{1,0:T(8,128)(2,1)S(1)}, bf16[2048,256]{1,0:T(8,128)(2,1)}, u32[]{:S(2)}) %copy-start.3) | copy-done | bytes 1048600
  7.5 0.0 copy-start.4
  7.5 1.0 %copy-done.4 = bf16[128,2048]{1,0:T(8,128)(2,1)S(1)} copy-done((bf16[128,2048]{1,0:T(8,128)(2,1)S(1)}, bf16[128,2048]{1,0:T(8,128)(2,1)}, u32[]{:S(2)}) %copy-start.4) | copy-done | bytes 524312
  8.5 0.0 copy-start.5
  8.5 0.7 copy-done.5
  9.2 29.3 %shard_map.118 = (bf16[1024,512]{1,0:T(8,128)(2,1)S(1)}, bf16[512,512]{1,0:T(8,128)(2,1)S(1)}) custom-call(bf16[128,2048]{1,0:T(8,128)(2,1)S(1)} %copy-done.4, f32[1,2048]{1,0:T(1,128)S(1)} %bitcast.3, bf16[2048,512]{1,0:T(8,128)(2,1)S(1)} %copy-done, bf16[2048,256]{1,0:T(8,128)(2,1)S(1)} %copy-done.2, bf16[2048,256]{1,0:T(8,128)(2,1)S(1)} %copy-done.3), custom_call_target="tpu_custom_call" | custom-call | tf_op jit(solution)/shard_map/pallas_call | solution.py:344
  38.5 0.0 copy-start.1
  38.5 31.9 %shard_map.119 = (bf16[1024,512]{1,0:T(8,128)(2,1)S(1)}, f32[8,8,128]{2,1,0:T(8,128)S(1)}) custom-call(s32[2,64]{1,0:T(2,128)S(1)} %select_reduce_fusion.1.entries, s32[2]{0:T(128)S(1)} %get-tuple-element.13.counts, s32[2]{0:T(128)S(1)} %pad_add_fusion.1.meta, bf16[1024,512]{1,0:T(8,128)(2,1)S(1)} %get-tuple-element.9.q_ref, ...), custom_call_target="tpu_custom_call" | custom-call | flops 8589934592 | bytes 8388608 | tf_op jit(solution)/shard_map/pallas_call | solution.py:131
  70.5 0.0 copy-done.1
  70.5 27.0 %shard_map.120 = bf16[128,512]{1,0:T(8,128)(2,1)S(1)} custom-call(bf16[1024,512]{1,0:T(8,128)(2,1)S(1)} %get-tuple-element.11.part_ref, f32[8,8,128]{2,1,0:T(8,128)S(1)} %get-tuple-element.12.ls_ref, bf16[512,2048]{1,0:T(8,128)(2,1)S(1)} %copy-done.1), custom_call_target="tpu_custom_call" | custom-call | tf_op jit(solution)/shard_map/pallas_call | solution.py:575
  97.5 0.7 copy.14
  (4 shorter events, 0.0 us)
Async XLA Ops:
  3.4 1.6 %copy-start = (bf16[2048,512]{1,0:T(8,128)(2,1)S(1)}, bf16[2048,512]{1,0:T(8,128)(2,1)}, u32[]{:S(2)}) copy-start(bf16[2048,512]{1,0:T(8,128)(2,1)} %wq_ref.1) | copy-start | bytes 6291460
  5.0 1.2 %copy-start.2 = (bf16[2048,256]{1,0:T(8,128)(2,1)S(1)}, bf16[2048,256]{1,0:T(8,128)(2,1)}, u32[]{:S(2)}) copy-start(bf16[2048,256]{1,0:T(8,128)(2,1)} %wk_ref.1) | copy-start | bytes 3145732
  6.2 1.2 %copy-start.3 = (bf16[2048,256]{1,0:T(8,128)(2,1)S(1)}, bf16[2048,256]{1,0:T(8,128)(2,1)}, u32[]{:S(2)}) copy-start(bf16[2048,256]{1,0:T(8,128)(2,1)} %wv_ref.1) | copy-start | bytes 3145732
  7.5 1.0 %copy-start.4 = (bf16[128,2048]{1,0:T(8,128)(2,1)S(1)}, bf16[128,2048]{1,0:T(8,128)(2,1)}, u32[]{:S(2)}) copy-start(bf16[128,2048]{1,0:T(8,128)(2,1)} %x_ref.1) | copy-start | bytes 1572868
  8.5 0.7 copy-start.5
  38.5 32.0 %copy-start.1 = (bf16[512,2048]{1,0:T(8,128)(2,1)S(1)}, bf16[512,2048]{1,0:T(8,128)(2,1)}, u32[]{:S(2)}) copy-start(bf16[512,2048]{1,0:T(8,128)(2,1)} %w_ref.1) | copy-start | bytes 6291460

commit v4 on v3

--- a/solution.py
+++ b/solution.py
@@ -22,6 +22,10 @@
 MESH = pl.DeviceIdType.MESH
 
 
+def in_hbm(array):
+    return pltpu.with_memory_space_constraint(array, pltpu.HBM)
+
+
 def dot_nt(left, right):
     return lax.dot_general(
         left, right, (((1,), (1,)), ((), ())), preferred_element_type=jnp.float32
@@ -35,16 +39,24 @@
     counts,
     meta,
     q_ref,
-    kn_ref,
-    vn_ref,
+    fresh_ref,
+    kc_hbm,
+    vc_hbm,
+    o_ref,
+    ls_ref,
     kc_ref,
     vc_ref,
-    o_ref,
-    ls_ref,
     m_ref,
     acc_ref,
+    load_sem,
 ):
-    request = pl.program_id(0)
+    loads = [
+        pltpu.make_async_copy(kc_hbm, kc_ref, load_sem.at[0]),
+        pltpu.make_async_copy(vc_hbm, vc_ref, load_sem.at[1]),
+    ]
+    for load in loads:
+        load.start()
+    total_rows = q_ref.shape[0]
     heads = m_ref.shape[0]
     kv_count = heads // per_kv
     ls_ref[...] = jnp.zeros_like(ls_ref)
@@ -54,54 +66,58 @@
     def cols(index):
         return slice(index * HEAD_DIM, (index + 1) * HEAD_DIM)
 
-    @pl.when(meta[0] == request)
-    def _():
-        start = pl.multiple_of(meta[1], tok_rows)
-        row = lax.broadcasted_iota(jnp.int32, (tok_rows, ADDED_TOKENS), 0)
-        col = lax.broadcasted_iota(jnp.int32, (tok_rows, ADDED_TOKENS), 1)
-        live = col <= row + start
-        ones = jnp.ones((ADDED_TOKENS, HEAD_DIM), jnp.bfloat16)
-        for head in range(heads):
-            kv = head // per_kv
-            scores = dot_nt(q_ref[pl.ds(start, tok_rows), cols(head)], kn_ref[:, cols(kv)])
-            scores = jnp.where(live, scores, EMPTY)
-            top = jnp.max(scores, axis=1, keepdims=True)
-            weights = jnp.exp2((scores - top) * EXP2_SCALE).astype(jnp.bfloat16)
-            values = jnp.concatenate([vn_ref[:, cols(kv)], ones], axis=1)
-            m_ref[head, pl.ds(start, tok_rows), :] = jnp.broadcast_to(top, (tok_rows, HEAD_DIM))
-            acc_ref[head, pl.ds(start, tok_rows), :] = jnp.dot(
-                weights, values, preferred_element_type=jnp.float32
+    start = pl.multiple_of(meta[0], tok_rows)
+    row = lax.broadcasted_iota(jnp.int32, (tok_rows, ADDED_TOKENS), 0)
+    col = lax.broadcasted_iota(jnp.int32, (tok_rows, ADDED_TOKENS), 1)
+    live = col <= row + meta[1]
+    ones = jnp.ones((ADDED_TOKENS, HEAD_DIM), jnp.bfloat16)
+    for head in range(heads):
+        kv = head // per_kv
+        scores = dot_nt(q_ref[pl.ds(start, tok_rows), cols(head)], fresh_ref[:, cols(kv)])
+        scores = jnp.where(live, scores, EMPTY)
+        top = jnp.max(scores, axis=1, keepdims=True)
+        weights = jnp.exp2((scores - top) * EXP2_SCALE).astype(jnp.bfloat16)
+        values = jnp.concatenate([fresh_ref[:, cols(kv_count + kv)], ones], axis=1)
+        m_ref[head, pl.ds(start, tok_rows), :] = jnp.broadcast_to(top, (tok_rows, HEAD_DIM))
+        acc_ref[head, pl.ds(start, tok_rows), :] = jnp.dot(
+            weights, values, preferred_element_type=jnp.float32
+        )
+    for load in loads:
+        load.wait()
+
+    def attend_request(request, carry):
+        def step(index, carry):
+            picked = [entries[request, index * STEP_PAGES + j] for j in range(STEP_PAGES)]
+            lane = lax.broadcasted_iota(jnp.int32, (1, PAGE_ROWS), 1)
+            bias = jnp.concatenate(
+                [jnp.where(lane < (item & 255), 0.0, EMPTY) for item in picked], axis=1
             )
-
-    def step(index, carry):
-        picked = [entries[request, index * STEP_PAGES + j] for j in range(STEP_PAGES)]
-        lane = lax.broadcasted_iota(jnp.int32, (1, PAGE_ROWS), 1)
-        bias = jnp.concatenate(
-            [jnp.where(lane < (item & 255), 0.0, EMPTY) for item in picked], axis=1
-        )
-        pages = [item >> 8 for item in picked]
-        ones = jnp.ones((STEP_PAGES * PAGE_ROWS, HEAD_DIM), jnp.bfloat16)
-        for kv in range(kv_count):
-            keys = jnp.concatenate([kc_ref[page, :, cols(kv)] for page in pages], axis=0)
-            values = jnp.concatenate([vc_ref[page, :, cols(kv)] for page in pages], axis=0)
-            values = jnp.concatenate([values, ones], axis=1)
-            for head in range(kv * per_kv, (kv + 1) * per_kv):
-                for chunk in range(ADDED_TOKENS // ROW_CHUNK):
-                    rows = slice(chunk * ROW_CHUNK, (chunk + 1) * ROW_CHUNK)
-                    scores = dot_nt(q_ref[rows, cols(head)], keys) + bias
-                    old = m_ref[head, rows, :]
-                    new = jnp.maximum(old, jnp.max(scores, axis=1, keepdims=True))
-                    weights = jnp.exp2(
-                        (scores - jnp.tile(new, (1, STEP_PAGES))) * EXP2_SCALE
-                    ).astype(jnp.bfloat16)
-                    keep = jnp.exp2((old - new) * EXP2_SCALE)
-                    m_ref[head, rows, :] = new
-                    acc_ref[head, rows, :] = acc_ref[head, rows, :] * jnp.tile(
-                        keep, (1, 2)
-                    ) + jnp.dot(weights, values, preferred_element_type=jnp.float32)
-        return carry
-
-    lax.fori_loop(0, (counts[request] + STEP_PAGES - 1) // STEP_PAGES, step, 0)
+            pages = [item >> 8 for item in picked]
+            ones = jnp.ones((STEP_PAGES * PAGE_ROWS, HEAD_DIM), jnp.bfloat16)
+            for kv in range(kv_count):
+                keys = jnp.concatenate([kc_ref[page, :, cols(kv)] for page in pages], axis=0)
+                values = jnp.concatenate([vc_ref[page, :, cols(kv)] for page in pages], axis=0)
+                values = jnp.concatenate([values, ones], axis=1)
+                for head in range(kv * per_kv, (kv + 1) * per_kv):
+                    for chunk in range(ADDED_TOKENS // ROW_CHUNK):
+                        first = request * ADDED_TOKENS + chunk * ROW_CHUNK
+                        rows = pl.ds(pl.multiple_of(first, ROW_CHUNK), ROW_CHUNK)
+                        scores = dot_nt(q_ref[rows, cols(head)], keys) + bias
+                        old = m_ref[head, rows, :]
+                        new = jnp.maximum(old, jnp.max(scores, axis=1, keepdims=True))
+                        weights = jnp.exp2(
+                            (scores - jnp.tile(new, (1, STEP_PAGES))) * EXP2_SCALE
+                        ).astype(jnp.bfloat16)
+                        keep = jnp.exp2((old - new) * EXP2_SCALE)
+                        m_ref[head, rows, :] = new
+                        acc_ref[head, rows, :] = acc_ref[head, rows, :] * jnp.tile(
+                            keep, (1, 2)
+                        ) + jnp.dot(weights, values, preferred_element_type=jnp.float32)
+            return carry
+
+        return lax.fori_loop(0, (counts[request] + STEP_PAGES - 1) // STEP_PAGES, step, carry)
+
+    lax.fori_loop(0, total_rows // ADDED_TOKENS, attend_request, 0)
     eye = lax.broadcasted_iota(jnp.int32, (128, 128), 0) == lax.broadcasted_iota(
         jnp.int32, (128, 128), 1
     )
@@ -109,7 +125,7 @@
         den = jnp.maximum(acc_ref[head, :, HEAD_DIM:], 1.0)
         o_ref[:, cols(head)] = (acc_ref[head, :, :HEAD_DIM] / den).astype(jnp.bfloat16)
         scale = m_ref[head] * SCORE_SCALE + jnp.log(den)
-        for block in range(ADDED_TOKENS // 128):
+        for block in range(total_rows // 128):
             part = scale[block * 128 : (block + 1) * 128]
             line = jnp.sum(jnp.where(eye, part, 0.0), axis=0, keepdims=True)
             for piece in range(128 // tok_rows):
@@ -119,51 +135,34 @@
 
 
 def attend(entries, counts, meta, queries, fresh, key_cache, value_cache, per_kv, tok_rows):
-    total_rows = queries.shape[0]
-    requests = total_rows // ADDED_TOKENS
-    kv_cols = key_cache.shape[2]
-    heads = kv_cols // HEAD_DIM * per_kv
-    q_cols = heads * HEAD_DIM
-    whole = pl.BlockSpec(
-        key_cache.shape, lambda r, e, c, m: (0, 0, 0), pipeline_mode=pl.Buffered(1)
-    )
-    pages = key_cache.shape[0]
+    total_rows, q_cols = queries.shape
+    pages, _, kv_cols = key_cache.shape
+    heads = q_cols // HEAD_DIM
+    vmem = pl.BlockSpec(memory_space=pltpu.VMEM)
+    smem = pl.BlockSpec(memory_space=pltpu.SMEM)
+    hbm = pl.BlockSpec(memory_space=pltpu.HBM)
     return pl.pallas_call(
         functools.partial(attend_kernel, per_kv, tok_rows),
         out_shape=(
             jax.ShapeDtypeStruct((total_rows, q_cols), jnp.bfloat16),
             jax.ShapeDtypeStruct((total_rows // tok_rows, LINES, tok_rows), jnp.float32),
         ),
-        grid_spec=pltpu.PrefetchScalarGridSpec(
-            num_scalar_prefetch=3,
-            grid=(requests,),
-            in_specs=[
-                pl.BlockSpec((ADDED_TOKENS, q_cols), lambda r, e, c, m: (r, 0)),
-                pl.BlockSpec((ADDED_TOKENS, kv_cols), lambda r, e, c, m: (0, 0)),
-                pl.BlockSpec((ADDED_TOKENS, kv_cols), lambda r, e, c, m: (0, 1)),
-                whole,
-                whole,
-            ],
-            out_specs=(
-                pl.BlockSpec((ADDED_TOKENS, q_cols), lambda r, e, c, m: (r, 0)),
-                pl.BlockSpec(
-                    (ADDED_TOKENS // tok_rows, LINES, tok_rows), lambda r, e, c, m: (r, 0, 0)
-                ),
-            ),
-            scratch_shapes=[
-                pltpu.VMEM((heads, ADDED_TOKENS, HEAD_DIM), jnp.float32),
-                pltpu.VMEM((heads, ADDED_TOKENS, 2 * HEAD_DIM), jnp.float32),
-            ],
-        ),
-        compiler_params=pltpu.CompilerParams(
-            dimension_semantics=("arbitrary",), vmem_limit_bytes=48 << 20
-        ),
+        in_specs=[smem, smem, smem, vmem, vmem, hbm, hbm],
+        out_specs=(vmem, vmem),
+        scratch_shapes=[
+            pltpu.VMEM(key_cache.shape, key_cache.dtype),
+            pltpu.VMEM(value_cache.shape, value_cache.dtype),
+            pltpu.VMEM((heads, total_rows, HEAD_DIM), jnp.float32),
+            pltpu.VMEM((heads, total_rows, 2 * HEAD_DIM), jnp.float32),
+            pltpu.SemaphoreType.DMA((2,)),
+        ],
+        compiler_params=pltpu.CompilerParams(vmem_limit_bytes=48 << 20),
         cost_estimate=pl.CostEstimate(
             flops=4 * pages * PAGE_ROWS * ADDED_TOKENS * q_cols,
             bytes_accessed=4 * pages * PAGE_ROWS * kv_cols,
             transcendentals=pages * PAGE_ROWS * ADDED_TOKENS * heads,
         ),
-    )(entries, counts, meta, queries, fresh, fresh, key_cache, value_cache)
+    )(entries, counts, meta, queries, fresh, in_hbm(key_cache), in_hbm(value_cache))
 
 
 def page_lists(cached_lengths, group_ids, prompt_pages, own_pages, pages_dev, seq_index):
@@ -235,6 +234,7 @@
     wq_buf,
     wk_buf,
     wv_buf,
+    x_buf,
     load_sem,
 ):
     tok_rows = x_ref.shape[0]
@@ -242,7 +242,7 @@
     loads = [
         pltpu.make_async_copy(source, target, load_sem.at[index])
         for index, (source, target) in enumerate(
-            ((wq_ref, wq_buf), (wk_ref, wk_buf), (wv_ref, wv_buf))
+            ((x_ref, x_buf), (wq_ref, wq_buf), (wk_ref, wk_buf), (wv_ref, wv_buf))
         )
     ]
     for load in loads:
@@ -270,12 +270,13 @@
 
     greet([twin] + [(line_peer(distance), tensor) for distance in range(1, outer)])
 
-    floats = x_ref[...].astype(jnp.float32)
+    loads[0].wait()
+    floats = x_buf[...].astype(jnp.float32)
     mean = jnp.mean(floats * floats, axis=-1, keepdims=True)
     normed = (floats * lax.rsqrt(mean + 1e-05) * gain_ref[...]).astype(jnp.bfloat16)
 
     mine = q_rows(me)
-    loads[0].wait()
+    loads[1].wait()
     q_ref[mine, :] = jnp.dot(normed, wq_buf[...], preferred_element_type=jnp.float32).astype(
         jnp.bfloat16
     )
@@ -291,8 +292,8 @@
     started.append(copy)
 
     mine = kv_rows(me)
-    loads[1].wait()
     loads[2].wait()
+    loads[3].wait()
     for start, weight in ((0, wk_buf), (kv_cols, wv_buf)):
         kv_ref[mine, start : start + kv_cols] = jnp.dot(
             normed, weight[...], preferred_element_type=jnp.float32
@@ -341,24 +342,31 @@
     q_cols, kv_cols = query_weight.shape[1], key_weight.shape[1]
     slots = pltpu.SemaphoreType.DMA((seq_count // 2,))
     vmem = pl.BlockSpec(memory_space=pltpu.VMEM)
+    hbm = pl.BlockSpec(memory_space=pltpu.HBM)
     return pl.pallas_call(
         functools.partial(gather_kernel, seq_count),
         out_shape=(
             jax.ShapeDtypeStruct((tok_rows * seq_count, q_cols), jnp.bfloat16),
             jax.ShapeDtypeStruct((ADDED_TOKENS, 2 * kv_cols), jnp.bfloat16),
         ),
-        in_specs=[vmem] * 2 + [pl.BlockSpec(memory_space=pltpu.HBM)] * 3,
+        in_specs=[hbm, vmem, hbm, hbm, hbm],
         out_specs=(vmem, vmem),
         scratch_shapes=[slots] * 8
         + [
             pltpu.VMEM(weight.shape, weight.dtype)
-            for weight in (query_weight, key_weight, value_weight)
+            for weight in (query_weight, key_weight, value_weight, hidden_in)
         ]
-        + [pltpu.SemaphoreType.DMA((3,))],
+        + [pltpu.SemaphoreType.DMA((4,))],
         compiler_params=pltpu.CompilerParams(
             collective_id=0, has_side_effects=True, vmem_limit_bytes=24 << 20
         ),
-    )(hidden_in, norm_gain.reshape(1, -1), query_weight, key_weight, value_weight)
+    )(
+        in_hbm(hidden_in),
+        norm_gain.reshape(1, -1),
+        in_hbm(query_weight),
+        in_hbm(key_weight),
+        in_hbm(value_weight),
+    )
 
 
 def finish_kernel(
@@ -625,7 +633,7 @@
     )
     my_start = seq_index * tok_rows
     home = my_start // ADDED_TOKENS
-    meta = jnp.stack([home, my_start - home * ADDED_TOKENS]).astype(jnp.int32)
+    meta = jnp.stack([my_start, my_start - home * ADDED_TOKENS]).astype(jnp.int32)
     partial_value, log_scale = attend(
         entries, counts, meta, queries, fresh, key_cache, value_cache, per_kv, tok_rows
     )

time: 96.4 us -> 94.5 us (0.980); the launches traced: 98.1 us -> 95.1 us
  local copies, waits for them, and re-layouts: 6.44 us -> 1.36 us
  Pallas kernels: 88.2 us -> 90.2 us
    unnamed x13 -> x5, local copies, waits for them, and re-layouts: 6.44 us -> 1.36 us
    pallas_call x1, Pallas kernels: 27 us -> 29.8 us  [finish(): pl.pallas_call(functools.partial(finish_kernel, seq_count, tensor_count),...]
where the time goes in v4:
time: 94.5 us; the launch traced here: 95.1 us
  Pallas kernels  90.2 us (95%)
  other arithmetic  3.41 us (4%)
  local copies, waits for them, and re-layouts  1.36 us (1%)
    pallas_call x1, Pallas kernels, attend(): pl.pallas_call(functools.partial(attend_kernel, per_kv, tok_rows), out_sh...  31.6 us
    pallas_call x1, Pallas kernels, finish(): pl.pallas_call(functools.partial(finish_kernel, seq_count, tensor_count),...  29.8 us
    pallas_call x1, Pallas kernels, gather(): pl.pallas_call(functools.partial(gather_kernel, seq_count), out_shape=(ja...  28.8 us

profile of v4, /device:TPU:0, one launch (start us, length us, event | category | flops | bytes accessed | tf_op | source)
XLA Modules:
  0.0 95.1 jit_solution(15044558427347184372)
XLA Ops:
  0.0 0.1 pad_add_fusion.1.meta
  0.1 0.7 broadcast_add_fusion
  0.7 0.7 compare_convert_fusion
  1.5 0.8 multiply_reduce_fusion
  2.2 0.9 convert_reduce_fusion
  3.1 0.2 select_reduce_fusion
  3.3 0.1 select_reduce_fusion.1.entries
  3.4 0.0 copy-start.1
  3.4 0.7 copy-done.1
  4.1 28.8 %shard_map.118 = (bf16[1024,512]{1,0:T(8,128)(2,1)S(1)}, bf16[512,512]{1,0:T(8,128)(2,1)S(1)}) custom-call(bf16[128,2048]{1,0:T(8,128)(2,1)} %x_ref.1, f32[1,2048]{1,0:T(1,128)S(1)} %bitcast.3, bf16[2048,512]{1,0:T(8,128)(2,1)} %wq_ref.1, bf16[2048,256]{1,0:T(8,128)(2,1)} %wk_ref.1, bf16[2048,256]{1,0:T(8,128)(2,1)} %wv_ref.1), custom_call_target="tpu_custom_call" | custom-call | tf_op jit(solution)/shard_map/pallas_call | solution.py:346
  32.9 0.0 copy-start
  32.9 31.6 %shard_map.119 = (bf16[1024,512]{1,0:T(8,128)(2,1)S(1)}, f32[8,8,128]{2,1,0:T(8,128)S(1)}) custom-call(s32[2,64]{1,0:T(2,128)S(1)} %select_reduce_fusion.1.entries, s32[2]{0:T(128)S(1)} %get-tuple-element.13.counts, s32[2]{0:T(128)S(1)} %pad_add_fusion.1.meta, bf16[1024,512]{1,0:T(8,128)(2,1)S(1)} %get-tuple-element.9.q_ref, ...), custom_call_target="tpu_custom_call" | custom-call | flops 8589934592 | bytes 8388608 | tf_op jit(solution)/shard_map/pallas_call | solution.py:144
  64.6 0.0 copy-done
  64.6 29.8 %shard_map.120 = bf16[128,512]{1,0:T(8,128)(2,1)S(1)} custom-call(bf16[1024,512]{1,0:T(8,128)(2,1)S(1)} %get-tuple-element.11.part_ref, f32[8,8,128]{2,1,0:T(8,128)S(1)} %get-tuple-element.12.ls_ref, bf16[512,2048]{1,0:T(8,128)(2,1)S(1)} %copy-done), custom_call_target="tpu_custom_call" | custom-call | tf_op jit(solution)/shard_map/pallas_call | solution.py:583
  94.4 0.7 copy.14
  (4 shorter events, 0.0 us)
Async XLA Ops:
  3.4 0.7 copy-start.1
  32.9 31.6 %copy-start = (bf16[512,2048]{1,0:T(8,128)(2,1)S(1)}, bf16[512,2048]{1,0:T(8,128)(2,1)}, u32[]{:S(2)}) copy-start(bf16[512,2048]{1,0:T(8,128)(2,1)} %w_ref.1) | copy-start | bytes 6291460

commit v5 on v4

--- a/solution.py
+++ b/solution.py
@@ -282,14 +282,14 @@
     )
     started = []
     own = q_ref.at[mine, :]
+    copy = remote(own, own, qy_send.at[0], qy_recv.at[0], twin)
+    copy.start()
+    started.append(copy)
     for distance in range(1, outer):
         peer = (line_peer(distance), tensor)
         copy = remote(own, own, q_send.at[distance], q_recv.at[distance], peer)
         copy.start()
         started.append(copy)
-    copy = remote(own, own, qy_send.at[0], qy_recv.at[0], twin)
-    copy.start()
-    started.append(copy)
 
     mine = kv_rows(me)
     loads[2].wait()

time: 94.5 us -> 90.8 us (0.961); the launches traced: 95.1 us -> 90.2 us
  Pallas kernels: 90.2 us -> 85.4 us
    pallas_call x1, Pallas kernels: 29.8 us -> 25 us  [finish(): pl.pallas_call(functools.partial(finish_kernel, seq_count, tensor_count),...]
where the time goes in v5:
time: 90.8 us; the launch traced here: 90.2 us
  Pallas kernels  85.4 us (94%)
  other arithmetic  3.41 us (4%)
  local copies, waits for them, and re-layouts  1.36 us (1%)
    pallas_call x1, Pallas kernels, attend(): pl.pallas_call(functools.partial(attend_kernel, per_kv, tok_rows), out_sh...  31.6 us
    pallas_call x1, Pallas kernels, gather(): pl.pallas_call(functools.partial(gather_kernel, seq_count), out_shape=(ja...  28.8 us
    pallas_call x1, Pallas kernels, finish(): pl.pallas_call(functools.partial(finish_kernel, seq_count, tensor_count),...  25 us

profile of v5, /device:TPU:0, one launch (start us, length us, event | category | flops | bytes accessed | tf_op | source)
XLA Modules:
  0.0 90.2 jit_solution(794906170629491047)
XLA Ops:
  0.0 0.1 pad_add_fusion.1.meta
  0.1 0.7 broadcast_add_fusion
  0.7 0.7 compare_convert_fusion
  1.5 0.8 multiply_reduce_fusion
  2.2 0.9 convert_reduce_fusion
  3.1 0.2 select_reduce_fusion
  3.3 0.1 select_reduce_fusion.1.entries
  3.4 0.0 copy-start.1
  3.4 0.7 copy-done.1
  4.1 28.8 %shard_map.118 = (bf16[1024,512]{1,0:T(8,128)(2,1)S(1)}, bf16[512,512]{1,0:T(8,128)(2,1)S(1)}) custom-call(bf16[128,2048]{1,0:T(8,128)(2,1)} %x_ref.1, f32[1,2048]{1,0:T(1,128)S(1)} %bitcast.3, bf16[2048,512]{1,0:T(8,128)(2,1)} %wq_ref.1, bf16[2048,256]{1,0:T(8,128)(2,1)} %wk_ref.1, bf16[2048,256]{1,0:T(8,128)(2,1)} %wv_ref.1), custom_call_target="tpu_custom_call" | custom-call | tf_op jit(solution)/shard_map/pallas_call | solution.py:346
  32.9 0.0 copy-start
  32.9 31.6 %shard_map.119 = (bf16[1024,512]{1,0:T(8,128)(2,1)S(1)}, f32[8,8,128]{2,1,0:T(8,128)S(1)}) custom-call(s32[2,64]{1,0:T(2,128)S(1)} %select_reduce_fusion.1.entries, s32[2]{0:T(128)S(1)} %get-tuple-element.13.counts, s32[2]{0:T(128)S(1)} %pad_add_fusion.1.meta, bf16[1024,512]{1,0:T(8,128)(2,1)S(1)} %get-tuple-element.9.q_ref, ...), custom_call_target="tpu_custom_call" | custom-call | flops 8589934592 | bytes 8388608 | tf_op jit(solution)/shard_map/pallas_call | solution.py:144
  64.6 0.0 copy-done
  64.6 25.0 %shard_map.120 = bf16[128,512]{1,0:T(8,128)(2,1)S(1)} custom-call(bf16[1024,512]{1,0:T(8,128)(2,1)S(1)} %get-tuple-element.11.part_ref, f32[8,8,128]{2,1,0:T(8,128)S(1)} %get-tuple-element.12.ls_ref, bf16[512,2048]{1,0:T(8,128)(2,1)S(1)} %copy-done), custom_call_target="tpu_custom_call" | custom-call | tf_op jit(solution)/shard_map/pallas_call | solution.py:583
  89.6 0.7 copy.14
  (4 shorter events, 0.0 us)
Async XLA Ops:
  3.4 0.7 copy-start.1
  32.9 31.6 %copy-start = (bf16[512,2048]{1,0:T(8,128)(2,1)S(1)}, bf16[512,2048]{1,0:T(8,128)(2,1)}, u32[]{:S(2)}) copy-start(bf16[512,2048]{1,0:T(8,128)(2,1)} %w_ref.1) | copy-start | bytes 6291460
